TPU v7x, 256 devices: a whole 4x4x8 slice. The times are simulated.
256 devices in a mesh: ep: 64 (over z, x, y_hi), tp: 4 (over y_lo, core).
Axes of the slice: x: 4, y: 4 (y_hi: 2, y_lo: 2; y = y_hi * 2 + y_lo), z: 8, core: 2. Of those that a mesh axis runs over, the one named last changes fastest.
Arguments:
- context: bfloat16 [8192, 4096], P('ep', 'tp'), may hold values from -6 to 6
- wo_proj: bfloat16 [4096, 4096], P('tp'), may hold values from -0.09375 to 0.09375
- residual: bfloat16 [8192, 4096], P(('ep', 'tp')), may hold values from -16 to 16
- norm_gain: bfloat16 [4096], replicated, may hold values from 0.25 to 1.75
- expert_ids: int32 [8192, 8], P(('ep', 'tp')), may hold values from 0 to 63, all different within a row; in each aligned block of 32 rows (0 to 31, 32 to 63, ...) at most 8 rows name the same one
- route_weights: float32 [8192, 8], P(('ep', 'tp')), may hold values from 0.1 to 1
- w_gate_up: bfloat16 [64, 2, 768, 4096], P('ep', None, 'tp'), may hold values from -0.09375 to 0.09375
- w_down: bfloat16 [64, 768, 4096], P('ep', 'tp'), may hold values from -0.21875 to 0.21875
Outputs:
- layer_out: bfloat16 [8192, 4096], P(('ep', 'tp'))
Inputs may be any that keep to these rules, and one draw needn't show every extreme that they name: `expert_ids`: within the routes of one device's 32 tokens no expert is named more than 8 times, a bound that some block reaches; a token names 8 different experts.
All inputs are finite; a program needn't handle non-finite values.
Results may differ from a plain program's by a relative error of at most 0.0085.
Values may be sent and summed in bfloat16 or wider, within the bound.
A program may use at most 128 MiB of HBM per device.

v0:
```python
import jax
import jax.numpy as jnp
from jax import lax
from jax.sharding import PartitionSpec as P


def local(context, wo_proj, residual, norm_gain, expert_ids, route_weights, w_gate_up, w_down):
    quarter_rows, model_width = residual.shape
    top_count = expert_ids.shape[1]
    exp_local = w_gate_up.shape[0]
    ep_size = lax.axis_size("ep")
    experts = exp_local * ep_size
    capacity = max(2, min(quarter_rows, 2 * quarter_rows * top_count // experts))
    attn = lax.psum_scatter(
        jnp.dot(context, wo_proj, preferred_element_type=jnp.float32),
        "tp",
        scatter_dimension=0,
        tiled=True,
    )
    hidden = residual.astype(jnp.float32) + attn
    inverse_rms = lax.rsqrt(jnp.mean(hidden * hidden, axis=1, keepdims=True) + 1e-06)
    normed = (hidden * inverse_rms * norm_gain.astype(jnp.float32)).astype(jnp.bfloat16)
    flat_ids = expert_ids.reshape(-1)
    onehot = (flat_ids[:, None] == jnp.arange(experts, dtype=jnp.int32)[None, :]).astype(jnp.int32)
    before = jnp.cumsum(onehot, axis=0, dtype=jnp.int32) - onehot
    position = jnp.sum(before * onehot, axis=1, dtype=jnp.int32)
    slot_ids = flat_ids * capacity + position
    slot_range = jnp.arange(experts * capacity, dtype=jnp.int32)
    selected = slot_range[:, None] == slot_ids[None, :]
    placement = jnp.any(
        selected.reshape(experts * capacity, quarter_rows, top_count), axis=2
    ).astype(jnp.bfloat16)
    send_rows = jnp.dot(placement, normed, preferred_element_type=jnp.float32).astype(jnp.bfloat16)
    send_rows = send_rows.reshape(ep_size, exp_local * capacity, model_width)
    received = lax.all_to_all(send_rows, "ep", split_axis=0, concat_axis=0, tiled=True)
    received = received.reshape(ep_size, exp_local, capacity, model_width)
    piece = lax.all_gather(received[None], "tp", axis=0, tiled=True)
    gate = jnp.einsum(
        "nsjcd,jfd->nsjcf", piece, w_gate_up[:, 0], preferred_element_type=jnp.float32
    )
    up_proj = jnp.einsum(
        "nsjcd,jfd->nsjcf", piece, w_gate_up[:, 1], preferred_element_type=jnp.float32
    )
    activated = (jax.nn.silu(gate) * up_proj).astype(jnp.bfloat16)
    partials = jnp.einsum("nsjcf,jfd->nsjcd", activated, w_down, preferred_element_type=jnp.float32)
    combined = lax.psum_scatter(
        partials.astype(jnp.bfloat16), "tp", scatter_dimension=0, tiled=True
    ).astype(jnp.float32)
    expert_out = combined[0].astype(jnp.bfloat16)
    returned = lax.all_to_all(
        expert_out.reshape(ep_size, exp_local * capacity, model_width),
        "ep",
        split_axis=0,
        concat_axis=0,
        tiled=True,
    )
    returned = returned.reshape(experts * capacity, model_width)
    token_slots = slot_ids.reshape(quarter_rows, top_count)
    mixture = jnp.zeros((quarter_rows, model_width), jnp.float32)
    for choice_index in range(top_count):
        picker = (slot_range[None, :] == token_slots[:, choice_index][:, None]).astype(jnp.bfloat16)
        picked = jnp.dot(picker, returned, preferred_element_type=jnp.float32)
        mixture = mixture + route_weights[:, choice_index : choice_index + 1] * picked
    return (hidden + mixture).astype(jnp.bfloat16)


def solution(mesh):
    in_specs = (
        P("ep", "tp"),
        P("tp", None),
        P(("ep", "tp"), None),
        P(),
        P(("ep", "tp"), None),
        P(("ep", "tp"), None),
        P("ep", None, "tp", None),
        P("ep", "tp", None),
    )
    out_specs = P(("ep", "tp"), None)
    return jax.shard_map(local, mesh=mesh, in_specs=in_specs, out_specs=out_specs, check_vma=False)
```

profile of v0, /device:TPU:1, one launch (start us, length us, event | category | flops | bytes accessed | tf_op | source)
XLA Modules:
  0.0 634.1 jit_solution(903657910014447604)
XLA Ops:
  6.5 0.0 reduce-scatter.3.cloned.1.call-start
  6.6 6.2 fusion.50
  12.8 0.0 all-gather.3.cloned.1.call-start
  12.9 0.1 copy.22
  12.9 0.1 eq.164
  13.0 0.1 eq.160
  13.2 0.6 reduce-window.6
  13.8 0.2 slice_reduce_fusion
  14.0 0.1 fusion.39
  14.1 0.1 reduce_sum.21
  14.2 0.2 fusion.34
  14.5 33.3 %reduce-scatter.3.cloned.1.call-done = f32[32,4096]{1,0:T(8,128)} async-done(((f32[128,4096]{1,0:T(8,128)}), f32[32,4096]{1,0:T(8,128)}) %reduce-scatter.3.cloned.1.call-update) | async-done | bytes 524304 | tf_op jit(solution)/shard_map/reduce_scatter | solution.py:14
  47.8 1.2 multiply_reduce_fusion
  49.0 2.4 fusion
  51.3 106.5 %all_to_all.10 = bf16[64,8,4096]{2,1,0:T(8,128)(2,1)} all-to-all(bf16[64,8,4096]{2,1,0:T(8,128)(2,1)S(1)} %fusion), channel_id=1, replica_groups=mesh['ep'=64,'tp'=4] {'ep'}, dimensions={0} | all-to-all | bytes 8388608 | tf_op jit(solution)/shard_map/all_to_all | solution.py:35
  157.8 0.0 all-gather.3.cloned.1.call-update
  157.9 0.2 reduce-scatter.5.cloned.1.call-start
  158.1 152.1 %all-gather.3.cloned.1.call-done = bf16[256,8,4096]{2,1,0:T(8,128)(2,1)} async-done(((bf16[64,8,4096]{2,1,0:T(8,128)(2,1)}), bf16[256,8,4096]{2,1,0:T(8,128)(2,1)}) %all-gather.3.cloned.1.call-update) | async-done | bytes 16777232 | tf_op jit(solution)/shard_map/all_gather | solution.py:37
  310.2 12.2 %fusion.23 = f32[4,64,8,192]{3,2,1,0:T(8,128)} fusion(bf16[4,64,8,4096]{3,2,1,0:T(8,128)(2,1)} %bitcast.130, bf16[1,2,192,4096]{3,2,1,0:T(8,128)(2,1)} %param.14), kind=kOutput, calls=%fused_computation.36 | convolution fusion | flops 3221225472 | bytes 19922944 | tf_op jit(solution)/shard_map/nsjcd,jfd->nsjcf/dot_general | solution.py:41
  322.4 23.8 %convert_bitcast_fusion = bf16[4,64,1,8,4096]{4,3,1,0,2:T(8,128)(2,1)} fusion(bf16[1,192,4096]{2,1,0:T(8,128)(2,1)S(1)} %copy-done, f32[4,64,8,192]{3,2,1,0:T(8,128)} %fusion.23, bf16[4,64,8,4096]{3,2,1,0:T(8,128)(2,1)} %bitcast.131, bf16[1,2,192,4096]{3,2,1,0:T(8,128)(2,1)} %param.14), kind=kOutput, calls=%fused_computation | convolution fusion | flops 6453198848 | bytes 38797312 | tf_op jit(solution)/shard_map/nsjcf,jfd->nsjcd/dot_general | solution.py:45
  346.2 149.9 %reduce-scatter.5.cloned.1.call-done = bf16[1,64,1,8,4096]{4,3,1,0,2:T(8,128)(2,1)} async-done(((bf16[4,64,1,8,4096]{4,3,1,0,2:T(8,128)(2,1)}), bf16[1,64,1,8,4096]{4,3,1,0,2:T(8,128)(2,1)}) %reduce-scatter.5.cloned.1.call-update) | async-done | bytes 4194320 | tf_op jit(solution)/shard_map/reduce_scatter | solution.py:46
  496.1 12.9 %all-to-all-start.1 = ((bf16[64,8,4096]{2,1,0:T(8,128)(2,1)}), bf16[64,8,4096]{2,1,0:T(8,128)(2,1)}, u32[]{:S(2)}, u32[]{:S(2)}) async-start(bf16[64,8,4096]{2,1,0:T(8,128)(2,1)} %bitcast.129), calls=%async_computation.3 | async-start | bytes 8388608 | tf_op jit(solution)/shard_map/all_to_all | solution.py:50
  509.0 0.3 slice_reduce_fusion.1
  509.3 92.9 %all-to-all-done.1 = bf16[64,8,4096]{2,1,0:T(8,128)(2,1)} async-done(((bf16[64,8,4096]{2,1,0:T(8,128)(2,1)}), bf16[64,8,4096]{2,1,0:T(8,128)(2,1)}, u32[]{:S(2)}, u32[]{:S(2)}) %all-to-all-start.1) | async-done | bytes 4194336 | tf_op jit(solution)/shard_map/all_to_all | solution.py:50
  602.3 3.0 convolution_multiply_fusion.7
  605.3 3.0 fusion.8
  608.3 3.0 fusion.7
  611.4 3.0 fusion.6
  614.5 3.0 fusion.5
  617.5 3.1 fusion.4
  620.6 3.2 fusion.3
  623.8 3.8 fusion.9
  (23 shorter events, 0.1 us)
Async XLA Ops:
  6.5 315.8 %copy-start = (bf16[1,192,4096]{2,1,0:T(8,128)(2,1)S(1)}, bf16[1,192,4096]{2,1,0:T(8,128)(2,1)}, u32[]{:S(2)}) copy-start(bf16[1,192,4096]{2,1,0:T(8,128)(2,1)} %param.15) | copy-start | bytes 4718596
  6.5 6.3 copy-start.5
  6.5 6.6 %copy-start.4 = (bf16[4096]{0:T(1024)(128)(2,1)S(1)}, bf16[4096]{0:T(1024)(128)(2,1)}, u32[]{:S(2)}) copy-start(bf16[4096]{0:T(1024)(128)(2,1)} %param.11) | copy-start | bytes 24580
  6.5 41.2 %copy-start.3 = (bf16[32,4096]{1,0:T(8,128)(2,1)S(1)}, bf16[32,4096]{1,0:T(8,128)(2,1)}, u32[]{:S(2)}) copy-start(bf16[32,4096]{1,0:T(8,128)(2,1)} %param.10) | copy-start | bytes 786436
  6.5 41.2 %reduce-scatter.3.cloned.1.call-start = ((), (), s32[]{:S(2)}) async-start(), calls=%async_computation.4 | async-start | bytes 2621440 | tf_op jit(solution)/shard_map/reduce_scatter | solution.py:14
  12.8 297.4 %all-gather.3.cloned.1.call-start = ((), (), s32[]{:S(2)}) async-start(), calls=%async_computation.6 | async-start | bytes 20971520 | tf_op jit(solution)/shard_map/all_gather | solution.py:37
  157.9 338.2 %reduce-scatter.5.cloned.1.call-start = ((), (), s32[]{:S(2)}) async-start(), calls=%async_computation.5 | async-start | bytes 20971520 | tf_op jit(solution)/shard_map/reduce_scatter | solution.py:46
  496.1 13.2 %copy-start.6 = (f32[32,8]{0,1:T(8,128)S(1)}, f32[32,8]{0,1:T(8,128)}, u32[]{:S(2)}) copy-start(f32[32,8]{0,1:T(8,128)} %param.13) | copy-start | bytes 3076
  496.1 106.2 %all-to-all-start.1 = ((bf16[64,8,4096]{2,1,0:T(8,128)(2,1)}), bf16[64,8,4096]{2,1,0:T(8,128)(2,1)}, u32[]{:S(2)}, u32[]{:S(2)}) async-start(bf16[64,8,4096]{2,1,0:T(8,128)(2,1)} %bitcast.129), calls=%async_computation.3 | async-start | bytes 8388608 | tf_op jit(solution)/shard_map/all_to_all | solution.py:50
  617.5 6.3 copy-start.2
  620.6 7.0 %copy-start.1 = (bf16[1,192,4096]{2,1,0:T(8,128)(2,1)S(1)}, bf16[1,192,4096]{2,1,0:T(8,128)(2,1)}, u32[]{:S(2)}) copy-start(bf16[1,192,4096]{2,1,0:T(8,128)(2,1)} %param.15) | copy-start | bytes 4718596
Sparse Core Ops, SparseCore 0:
  12.9 34.7 reduce-scatter.2
  158.0 152.1 all-gather.2
  346.3 149.7 reduce-scatter.4
where the time goes:
time: 637 us; the launch traced here: 634 us
  waiting for transfers between devices  428 us (67%)
  blocking collectives  106 us (17%)
  matrix products  69.8 us (11%)
  between operations  13.3 us (2%)
  starting transfers between devices  13.2 us (2%)
    all_gather x1, waiting for transfers between devices, local(): piece = lax.all_gather(received[None], 'tp', axis=0, tiled=True)  152 us
    reduce_scatter x1, waiting for transfers between devices, local(): lax.psum_scatter(partials.astype(jnp.bfloat16), 'tp', scatter_dimension=0...  150 us
    all_to_all x1, blocking collectives, local(): lax.all_to_all(send_rows, 'ep', split_axis=0, concat_axis=0, tiled=True)  106 us
    all_to_all x1, waiting for transfers between devices, local(): lax.all_to_all(expert_out.reshape(ep_size, exp_local * capacity, model_wi...  92.9 us
    reduce_scatter x1, waiting for transfers between devices, local(): lax.psum_scatter(jnp.dot(context, wo_proj, preferred_element_type=jnp.flo...  33.3 us
    dot_general x8, matrix products, local(): picked = jnp.dot(picker, returned, preferred_element_type=jnp.float32)  25.3 us
    dot_general x1, matrix products, local(): jnp.einsum('nsjcf,jfd->nsjcd', activated, w_down, preferred_element_type=...  23.8 us
    all_to_all x1, starting transfers between devices, local(): lax.all_to_all(expert_out.reshape(ep_size, exp_local * capacity, model_wi...  12.9 us
  transfers between devices with their start and end apart: 4, of which 4 were waited for; matrix products, arithmetic and copies ran while one was open for 0% of the time, Pallas kernels for 0%

commit v1 on v0

--- a/solution.py
+++ b/solution.py
@@ -11,6 +11,8 @@
     ep_size = lax.axis_size("ep")
     experts = exp_local * ep_size
     capacity = max(2, min(quarter_rows, 2 * quarter_rows * top_count // experts))
+    gate_up_full = lax.all_gather(w_gate_up, "tp", axis=2, tiled=True)
+    down_full = lax.all_gather(w_down, "tp", axis=1, tiled=True)
     attn = lax.psum_scatter(
         jnp.dot(context, wo_proj, preferred_element_type=jnp.float32),
         "tp",
@@ -34,19 +36,16 @@
     send_rows = send_rows.reshape(ep_size, exp_local * capacity, model_width)
     received = lax.all_to_all(send_rows, "ep", split_axis=0, concat_axis=0, tiled=True)
     received = received.reshape(ep_size, exp_local, capacity, model_width)
-    piece = lax.all_gather(received[None], "tp", axis=0, tiled=True)
     gate = jnp.einsum(
-        "nsjcd,jfd->nsjcf", piece, w_gate_up[:, 0], preferred_element_type=jnp.float32
+        "sjcd,jfd->sjcf", received, gate_up_full[:, 0], preferred_element_type=jnp.float32
     )
     up_proj = jnp.einsum(
-        "nsjcd,jfd->nsjcf", piece, w_gate_up[:, 1], preferred_element_type=jnp.float32
+        "sjcd,jfd->sjcf", received, gate_up_full[:, 1], preferred_element_type=jnp.float32
     )
     activated = (jax.nn.silu(gate) * up_proj).astype(jnp.bfloat16)
-    partials = jnp.einsum("nsjcf,jfd->nsjcd", activated, w_down, preferred_element_type=jnp.float32)
-    combined = lax.psum_scatter(
-        partials.astype(jnp.bfloat16), "tp", scatter_dimension=0, tiled=True
-    ).astype(jnp.float32)
-    expert_out = combined[0].astype(jnp.bfloat16)
+    expert_out = jnp.einsum(
+        "sjcf,jfd->sjcd", activated, down_full, preferred_element_type=jnp.float32
+    ).astype(jnp.bfloat16)
     returned = lax.all_to_all(
         expert_out.reshape(ep_size, exp_local * capacity, model_width),
         "ep",

time: 637 us -> 445 us (0.70)
  waiting for transfers between devices: 428 us -> 250 us
  matrix products: 69.8 us -> 57.2 us
    reduce_scatter x1 -> x0, waiting for transfers between devices: 150 us -> none  [local(): lax.psum_scatter(partials.astype(jnp.bfloat16), 'tp', scatter_dimension=0...]
    all_gather x1 -> x2, waiting for transfers between devices: 152 us -> 116 us  [the longest x1 62 us: local(): down_full = lax.all_gather(w_down, 'tp', axis=1, tiled=True)]
    dot_general x2, matrix products: 36 us -> 23.7 us  [the longest x1 16.6 us: local(): jnp.einsum('sjcf,jfd->sjcd', activated, down_full, preferred_element_type...]
    all_to_all x1, waiting for transfers between devices: 92.9 us -> 101 us  [local(): lax.all_to_all(expert_out.reshape(ep_size, exp_local * capacity, model_wi...]
  transfers between devices with their start and end apart: 4 -> 4, of which waited for: 4 -> 4; matrix products, arithmetic and copies ran while one was open for 0% -> 3% of each run, Pallas kernels for 0% -> 0%
where the time goes in v1:
time: 445 us; the launch traced here: 444 us
  waiting for transfers between devices  250 us (56%)
  blocking collectives  107 us (24%)
  matrix products  57.2 us (13%)
  between operations  13.3 us (3%)
  starting transfers between devices  13 us (3%)
    all_to_all x1, blocking collectives, local(): lax.all_to_all(send_rows, 'ep', split_axis=0, concat_axis=0, tiled=True)  107 us
    all_to_all x1, waiting for transfers between devices, local(): lax.all_to_all(expert_out.reshape(ep_size, exp_local * capacity, model_wi...  101 us
    all_gather x1, waiting for transfers between devices, local(): down_full = lax.all_gather(w_down, 'tp', axis=1, tiled=True)  62 us
    all_gather x1, waiting for transfers between devices, local(): gate_up_full = lax.all_gather(w_gate_up, 'tp', axis=2, tiled=True)  53.6 us
    reduce_scatter x1, waiting for transfers between devices, local(): lax.psum_scatter(jnp.dot(context, wo_proj, preferred_element_type=jnp.flo...  31.9 us
    dot_general x8, matrix products, local(): picked = jnp.dot(picker, returned, preferred_element_type=jnp.float32)  25.1 us
    dot_general x1, matrix products, local(): jnp.einsum('sjcf,jfd->sjcd', activated, down_full, preferred_element_type...  16.6 us
    all_to_all x1, starting transfers between devices, local(): lax.all_to_all(expert_out.reshape(ep_size, exp_local * capacity, model_wi...  12.9 us
  transfers between devices with their start and end apart: 4, of which 4 were waited for; matrix products, arithmetic and copies ran while one was open for 3% of the time, Pallas kernels for 0%

profile of v1, /device:TPU:1, one launch (start us, length us, event | category | flops | bytes accessed | tf_op | source)
XLA Modules:
  0.0 444.3 jit_solution(16430905282046604405)
XLA Ops:
  6.5 0.9 copy-done
  7.5 5.9 %fusion.47 = f32[128,4096]{1,0:T(8,128)} fusion(bf16[128,1024]{1,0:T(8,128)(2,1)S(1)} %copy-done, bf16[1024,4096]{1,0:T(8,128)(2,1)} %param.9), kind=kOutput, calls=%fused_computation.94 | convolution fusion | flops 1073741824 | bytes 10747904 | tf_op jit(solution)/shard_map/dot_general | solution.py:17
  13.5 0.0 all-gather.3.cloned.1.call-start
  13.5 0.7 all-gather.3.cloned.1.call-update
  14.3 0.7 all-gather.5.cloned.1.call-update
  15.0 0.1 copy.18
  15.0 0.1 eq.164
  15.1 0.1 eq.160
  15.3 0.6 reduce-window.6
  15.9 0.2 slice_reduce_fusion
  16.1 0.1 fusion.36
  16.2 0.1 reduce_sum.21
  16.3 0.2 fusion.31
  16.5 31.9 %reduce-scatter.2.cloned.1.call-done = f32[32,4096]{1,0:T(8,128)} async-done(((f32[128,4096]{1,0:T(8,128)}), f32[32,4096]{1,0:T(8,128)}) %reduce-scatter.2.cloned.1.call-update) | async-done | bytes 524304 | tf_op jit(solution)/shard_map/reduce_scatter | solution.py:16
  48.4 1.2 multiply_reduce_fusion
  49.6 2.4 fusion.7
  52.0 106.6 %all_to_all.10 = bf16[64,8,4096]{2,1,0:T(8,128)(2,1)} all-to-all(bf16[64,8,4096]{2,1,0:T(8,128)(2,1)S(1)} %fusion.7), channel_id=1, replica_groups=mesh['ep'=64,'tp'=4] {'ep'}, dimensions={0} | all-to-all | bytes 8388608 | tf_op jit(solution)/shard_map/all_to_all | solution.py:37
  158.6 53.6 %all-gather.3.cloned.1.call-done = bf16[1,2,768,4096]{3,2,1,0:T(8,128)(2,1)} async-done(((bf16[1,2,192,4096]{3,2,1,0:T(8,128)(2,1)}), bf16[1,2,768,4096]{3,2,1,0:T(8,128)(2,1)}) %all-gather.3.cloned.1.call-update) | async-done | bytes 12582928 | tf_op jit(solution)/shard_map/all_gather | solution.py:14
  212.2 7.1 %fusion.1 = f32[64,8,768]{2,1,0:T(8,128)S(1)} fusion(bf16[64,8,4096]{2,1,0:T(8,128)(2,1)} %all_to_all.10, bf16[1,2,768,4096]{3,2,1,0:T(8,128)(2,1)} %all-gather.3.cloned.1.call-done), kind=kOutput, calls=%fused_computation.3 | convolution fusion | flops 3221225472 | bytes 12058624 | tf_op jit(solution)/shard_map/sjcd,jfd->sjcf/dot_general | solution.py:39
  219.3 62.0 %all-gather.5.cloned.1.call-done = bf16[1,768,4096]{2,1,0:T(8,128)(2,1)} async-done(((bf16[1,192,4096]{2,1,0:T(8,128)(2,1)}), bf16[1,768,4096]{2,1,0:T(8,128)(2,1)}) %all-gather.5.cloned.1.call-update) | async-done | bytes 6291472 | tf_op jit(solution)/shard_map/all_gather | solution.py:15
  281.3 16.6 %fusion.4 = bf16[64,8,4096]{2,1,0:T(8,128)(2,1)} fusion(bf16[1,768,4096]{2,1,0:T(8,128)(2,1)} %all-gather.5.cloned.1.call-done, bf16[64,8,4096]{2,1,0:T(8,128)(2,1)} %all_to_all.10, bf16[1,2,768,4096]{3,2,1,0:T(8,128)(2,1)} %all-gather.3.cloned.1.call-done, f32[64,8,768]{2,1,0:T(8,128)S(1)} %fusion.1), kind=kOutput, calls=%fused_computation.6 | convolution fusion | flops 6446907392 | bytes 22544384 | tf_op jit(solution)/shard_map/sjcf,jfd->sjcd/dot_general | solution.py:46
  297.9 12.9 %all-to-all-start.1 = ((bf16[64,8,4096]{2,1,0:T(8,128)(2,1)}), bf16[64,8,4096]{2,1,0:T(8,128)(2,1)}, u32[]{:S(2)}, u32[]{:S(2)}) async-start(bf16[64,8,4096]{2,1,0:T(8,128)(2,1)} %fusion.4), calls=%async_computation.2 | async-start | bytes 8388608 | tf_op jit(solution)/shard_map/all_to_all | solution.py:49
  310.8 0.3 slice_reduce_fusion.1
  311.2 101.4 %all-to-all-done.1 = bf16[64,8,4096]{2,1,0:T(8,128)(2,1)} async-done(((bf16[64,8,4096]{2,1,0:T(8,128)(2,1)}), bf16[64,8,4096]{2,1,0:T(8,128)(2,1)}, u32[]{:S(2)}, u32[]{:S(2)}) %all-to-all-start.1) | async-done | bytes 4194336 | tf_op jit(solution)/shard_map/all_to_all | solution.py:49
  412.5 3.0 convolution_multiply_fusion.7
  415.6 3.0 fusion.15
  418.6 3.0 fusion.14
  421.7 3.0 fusion.13
  424.7 3.0 fusion.12
  427.8 3.1 fusion.11
  430.9 3.0 fusion.10
  434.0 3.8 fusion.16
  (21 shorter events, 0.2 us)
Async XLA Ops:
  6.5 1.0 copy-start
  6.5 41.9 %reduce-scatter.2.cloned.1.call-start = ((), (), s32[]{:S(2)}) async-start(), calls=%async_computation.3 | async-start | bytes 2621440 | tf_op jit(solution)/shard_map/reduce_scatter | solution.py:16
  13.4 1.5 copy-start.4
  13.4 1.8 copy-start.3
  13.4 35.0 %copy-start.2 = (bf16[32,4096]{1,0:T(8,128)(2,1)S(1)}, bf16[32,4096]{1,0:T(8,128)(2,1)}, u32[]{:S(2)}) copy-start(bf16[32,4096]{1,0:T(8,128)(2,1)} %param.10) | copy-start | bytes 786436
  13.5 198.7 %all-gather.3.cloned.1.call-start = ((), (), s32[]{:S(2)}) async-start(), calls=%async_computation.4 | async-start | bytes 15728640 | tf_op jit(solution)/shard_map/all_gather | solution.py:14
  14.2 267.1 %all-gather.5.cloned.1.call-start = ((), (), s32[]{:S(2)}) async-start(), calls=%async_computation.5 | async-start | bytes 7864320 | tf_op jit(solution)/shard_map/all_gather | solution.py:15
  297.9 13.2 %copy-start.5 = (f32[32,8]{0,1:T(8,128)S(1)}, f32[32,8]{0,1:T(8,128)}, u32[]{:S(2)}) copy-start(f32[32,8]{0,1:T(8,128)} %param.13) | copy-start | bytes 3076
  297.9 114.6 %all-to-all-start.1 = ((bf16[64,8,4096]{2,1,0:T(8,128)(2,1)}), bf16[64,8,4096]{2,1,0:T(8,128)(2,1)}, u32[]{:S(2)}, u32[]{:S(2)}) async-start(bf16[64,8,4096]{2,1,0:T(8,128)(2,1)} %fusion.4), calls=%async_computation.2 | async-start | bytes 8388608 | tf_op jit(solution)/shard_map/all_to_all | solution.py:49
  427.8 6.2 %copy-start.1 = (f32[32,4096]{1,0:T(8,128)S(1)}, f32[32,4096]{1,0:T(8,128)}, u32[]{:S(2)}) copy-start(f32[32,4096]{1,0:T(8,128)} %reduce-scatter.2.cloned.1.call-done) | copy-start | bytes 1572868
Sparse Core Ops, SparseCore 0:
  13.6 34.7 reduce-scatter.1
  50.2 161.9 all-gather.2
  214.0 67.2 all-gather.4

commit v2 on v1

--- a/solution.py
+++ b/solution.py
@@ -2,6 +2,17 @@
 import jax.numpy as jnp
 from jax import lax
 from jax.sharding import PartitionSpec as P
+
+
+def gather_weights(w_gate_up, w_down):
+    tp_size = lax.axis_size("tp")
+    half = tp_size // 2
+    far_pairs = [(j, j ^ half) for j in range(tp_size)]
+    near_pairs = [(j, j ^ 1) for j in range(tp_size)]
+    own = (w_gate_up, w_down)
+    far = lax.ppermute(own, "tp", far_pairs)
+    near_own, near_far = lax.ppermute((own, far), "tp", near_pairs)
+    return [own, far, near_own, near_far]
 
 
 def local(context, wo_proj, residual, norm_gain, expert_ids, route_weights, w_gate_up, w_down):
@@ -11,8 +22,7 @@
     ep_size = lax.axis_size("ep")
     experts = exp_local * ep_size
     capacity = max(2, min(quarter_rows, 2 * quarter_rows * top_count // experts))
-    gate_up_full = lax.all_gather(w_gate_up, "tp", axis=2, tiled=True)
-    down_full = lax.all_gather(w_down, "tp", axis=1, tiled=True)
+    pieces = gather_weights(w_gate_up, w_down)
     attn = lax.psum_scatter(
         jnp.dot(context, wo_proj, preferred_element_type=jnp.float32),
         "tp",
@@ -36,13 +46,14 @@
     send_rows = send_rows.reshape(ep_size, exp_local * capacity, model_width)
     received = lax.all_to_all(send_rows, "ep", split_axis=0, concat_axis=0, tiled=True)
     received = received.reshape(ep_size, exp_local, capacity, model_width)
-    gate = jnp.einsum(
-        "sjcd,jfd->sjcf", received, gate_up_full[:, 0], preferred_element_type=jnp.float32
-    )
-    up_proj = jnp.einsum(
-        "sjcd,jfd->sjcf", received, gate_up_full[:, 1], preferred_element_type=jnp.float32
-    )
-    activated = (jax.nn.silu(gate) * up_proj).astype(jnp.bfloat16)
+    activated = []
+    for gate_up_piece, _ in pieces:
+        both = jnp.einsum(
+            "sjcd,jgfd->sjcgf", received, gate_up_piece, preferred_element_type=jnp.float32
+        )
+        activated.append((jax.nn.silu(both[:, :, :, 0]) * both[:, :, :, 1]).astype(jnp.bfloat16))
+    activated = jnp.concatenate(activated, axis=3)
+    down_full = jnp.concatenate([down_piece for _, down_piece in pieces], axis=1)
     expert_out = jnp.einsum(
         "sjcf,jfd->sjcd", activated, down_full, preferred_element_type=jnp.float32
     ).astype(jnp.bfloat16)
@@ -55,11 +66,16 @@
     )
     returned = returned.reshape(experts * capacity, model_width)
     token_slots = slot_ids.reshape(quarter_rows, top_count)
-    mixture = jnp.zeros((quarter_rows, model_width), jnp.float32)
+    combine = jnp.zeros((quarter_rows, experts * capacity), jnp.float32)
     for choice_index in range(top_count):
-        picker = (slot_range[None, :] == token_slots[:, choice_index][:, None]).astype(jnp.bfloat16)
-        picked = jnp.dot(picker, returned, preferred_element_type=jnp.float32)
-        mixture = mixture + route_weights[:, choice_index : choice_index + 1] * picked
+        hit = slot_range[None, :] == token_slots[:, choice_index][:, None]
+        combine = combine + jnp.where(hit, route_weights[:, choice_index : choice_index + 1], 0.0)
+    combine_hi = combine.astype(jnp.bfloat16)
+    combine_lo = (combine - combine_hi.astype(jnp.float32)).astype(jnp.bfloat16)
+    picked = jnp.dot(
+        jnp.concatenate([combine_hi, combine_lo], axis=0), returned, preferred_element_type=jnp.float32
+    )
+    mixture = picked[:quarter_rows] + picked[quarter_rows:]
     return (hidden + mixture).astype(jnp.bfloat16)
 
 

time: 445 us -> 370 us (0.83)
  blocking collectives: 107 us -> 0 us
  waiting for transfers between devices: 250 us -> 274 us
  starting transfers between devices: 13 us -> 30.2 us
  matrix products: 57.2 us -> 40.1 us
    ppermute x0 -> x6, waiting for transfers between devices: none -> 146 us  [the longest x2 146 us: gather_weights(): far = lax.ppermute(own, 'tp', far_pairs)]
    all_gather x2 -> x0, waiting for transfers between devices: 116 us -> none  [the longest x1 62 us: local(): down_full = lax.all_gather(w_down, 'tp', axis=1, tiled=True)]
    all_to_all x1 -> x0, blocking collectives: 107 us -> none  [local(): lax.all_to_all(send_rows, 'ep', split_axis=0, concat_axis=0, tiled=True)]
    all_to_all x0 -> x1, starting transfers between devices: none -> 12.7 us  [local(): lax.all_to_all(send_rows, 'ep', split_axis=0, concat_axis=0, tiled=True)]
    dot_general x1, matrix products: 16.6 us -> 5.49 us  [local(): jnp.einsum('sjcf,jfd->sjcd', activated, down_full, preferred_element_type...]
    dot_general x9 -> x5, matrix products: 32.2 us -> 24.2 us  [the longest x4 21.2 us: local(): jnp.einsum('sjcd,jgfd->sjcgf', received, gate_up_piece, preferred_element...]
    all_to_all x1, waiting for transfers between devices: 101 us -> 94 us  [local(): lax.all_to_all(expert_out.reshape(ep_size, exp_local * capacity, model_wi...]
    ppermute x0 -> x6, starting transfers between devices: none -> 4.73 us  [the longest x4 3.22 us: gather_weights(): near_own, near_far = lax.ppermute((own, far), 'tp', near_pairs)]
  transfers between devices with their start and end apart: 4 -> 9, of which waited for: 4 -> 4; matrix products, arithmetic and copies ran while one was open for 3% -> 7% of each run, Pallas kernels for 0% -> 0%
where the time goes in v2:
time: 370 us; the launch traced here: 368 us
  waiting for transfers between devices  274 us (74%)
  matrix products  40.1 us (11%)
  starting transfers between devices  30.2 us (8%)
  between operations  13.6 us (4%)
  local copies, waits for them, and re-layouts  6.04 us (2%)
  other arithmetic  4.16 us (1%)
    ppermute x2, waiting for transfers between devices, gather_weights(): far = lax.ppermute(own, 'tp', far_pairs)  146 us
    all_to_all x1, waiting for transfers between devices, local(): lax.all_to_all(expert_out.reshape(ep_size, exp_local * capacity, model_wi...  94 us
    reduce_scatter x1, waiting for transfers between devices, local(): lax.psum_scatter(jnp.dot(context, wo_proj, preferred_element_type=jnp.flo...  33.4 us
    dot_general x4, matrix products, local(): jnp.einsum('sjcd,jgfd->sjcgf', received, gate_up_piece, preferred_element...  21.2 us
    all_to_all x1, starting transfers between devices, local(): lax.all_to_all(expert_out.reshape(ep_size, exp_local * capacity, model_wi...  12.7 us
    all_to_all x1, starting transfers between devices, local(): lax.all_to_all(send_rows, 'ep', split_axis=0, concat_axis=0, tiled=True)  12.7 us
  transfers between devices with their start and end apart: 9, of which 4 were waited for; matrix products, arithmetic and copies ran while one was open for 7% of the time, Pallas kernels for 0%

profile of v2, /device:TPU:1, one launch (start us, length us, event | category | flops | bytes accessed | tf_op | source)
XLA Modules:
  0.0 367.7 jit_solution(2199551659407201962)
XLA Ops:
  6.6 0.9 copy-done
  7.5 6.0 %fusion.69 = f32[128,4096]{1,0:T(8,128)} fusion(bf16[128,1024]{1,0:T(8,128)(2,1)S(1)} %copy-done, bf16[1024,4096]{1,0:T(8,128)(2,1)} %param.9), kind=kOutput, calls=%fused_computation.101 | convolution fusion | flops 1073741824 | bytes 10747904 | tf_op jit(solution)/shard_map/dot_general | solution.py:27
  13.8 0.6 reduce-window.6
  14.4 0.2 slice_reduce_fusion
  14.9 0.2 fusion.55
  15.1 33.4 %reduce-scatter.2.cloned.1.call-done = f32[32,4096]{1,0:T(8,128)} async-done(((f32[128,4096]{1,0:T(8,128)}), f32[32,4096]{1,0:T(8,128)}) %reduce-scatter.2.cloned.1.call-update) | async-done | bytes 524304 | tf_op jit(solution)/shard_map/reduce_scatter | solution.py:26
  48.5 1.2 multiply_reduce_fusion
  49.7 4.3 %fusion.9 = bf16[64,8,4096]{2,1,0:T(8,128)(2,1)} fusion(pred[512,32]{0,1:T(8,128)(4,1)S(1)} %fusion.55, f32[4096]{0:T(1024)S(1)} %convert_element_type.91, f32[32]{0:T(128)S(1)} %add_rsqrt_fusion, f32[32,4096]{1,0:T(8,128)} %reduce-scatter.2.cloned.1.call-done, bf16[32,4096]{1,0:T(8,128)(2,1)S(1)} %copy-done.2), kind=kOutput, calls=%fused_computation.11 | convolution fusion | flops 136970240 | bytes 5013632 | tf_op jit(solution)/shard_map/dot_general | solution.py:45
  54.0 12.7 %all-to-all-start = ((bf16[64,8,4096]{2,1,0:T(8,128)(2,1)}), bf16[64,8,4096]{2,1,0:T(8,128)(2,1)}, u32[]{:S(2)}, u32[]{:S(2)}) async-start(bf16[64,8,4096]{2,1,0:T(8,128)(2,1)} %fusion.9), calls=%async_computation.1 | async-start | bytes 8388608 | tf_op jit(solution)/shard_map/all_to_all | solution.py:47
  66.9 112.8 %collective-permute-done.3 = bf16[1,2,192,4096]{3,2,1,0:T(8,128)(2,1)} collective-permute-done((bf16[1,2,192,4096]{3,2,1,0:T(8,128)(2,1)}, bf16[1,2,192,4096]{3,2,1,0:T(8,128)(2,1)}, u32[]{:S(2)}, u32[]{:S(2)}) %collective-permute-start.3) | collective-permute-done | bytes 3145760 | tf_op jit(solution)/shard_map/ppermute | solution.py:13
  179.7 1.1 collective-permute-start.5
  180.8 1.4 collective-permute-start
  182.2 0.8 collective-permute-start.1
  183.0 33.3 %collective-permute-done = bf16[1,192,4096]{2,1,0:T(8,128)(2,1)} collective-permute-done((bf16[1,192,4096]{2,1,0:T(8,128)(2,1)S(1)}, bf16[1,192,4096]{2,1,0:T(8,128)(2,1)}, u32[]{:S(2)}, u32[]{:S(2)}) %collective-permute-start) | collective-permute-done | bytes 1572896 | tf_op jit(solution)/shard_map/ppermute | solution.py:13
  216.3 1.4 collective-permute-start.2
  217.7 5.5 %fusion.29 = f32[64,1,8,2,192]{4,2,0,3,1:T(8,128)S(1)} fusion(bf16[1,2,192,4096]{3,2,1,0:T(8,128)(2,1)} %collective-permute-done.3, bf16[64,8,4096]{2,1,0:T(8,128)(2,1)} %all-to-all-done), kind=kOutput, calls=%fused_computation.27 | convolution fusion | flops 1610612736 | bytes 8126464 | tf_op jit(solution)/shard_map/sjcd,jgfd->sjcgf/dot_general | solution.py:51
  223.2 5.5 %fusion.24 = f32[64,1,8,2,192]{4,2,0,3,1:T(8,128)S(1)} fusion(bf16[1,2,192,4096]{3,2,1,0:T(8,128)(2,1)} %collective-permute-done.5, bf16[64,8,4096]{2,1,0:T(8,128)(2,1)} %all-to-all-done), kind=kOutput, calls=%fused_computation.26 | convolution fusion | flops 1610612736 | bytes 8126464 | tf_op jit(solution)/shard_map/sjcd,jgfd->sjcgf/dot_general | solution.py:51
  228.8 5.6 %fusion.34 = f32[64,1,8,2,192]{4,2,0,3,1:T(8,128)S(1)} fusion(bf16[1,2,192,4096]{3,2,1,0:T(8,128)(2,1)} %collective-permute-done.4, bf16[64,8,4096]{2,1,0:T(8,128)(2,1)} %all-to-all-done), kind=kOutput, calls=%fused_computation.28 | convolution fusion | flops 1610612736 | bytes 8126464 | tf_op jit(solution)/shard_map/sjcd,jgfd->sjcgf/dot_general | solution.py:51
  234.4 0.2 fusion.48
  234.6 0.2 fusion.52
  234.8 0.2 fusion.50
  234.9 4.5 %fusion.39 = f32[64,1,8,2,192]{4,2,3,0,1:T(8,128)S(1)} fusion(bf16[1,2,192,4096]{3,2,1,0:T(8,128)(2,1)S(1)} %copy-done.6, bf16[64,8,4096]{2,1,0:T(8,128)(2,1)} %all-to-all-done), kind=kOutput, calls=%fused_computation.29 | convolution fusion | flops 1610612736 | bytes 8126464 | tf_op jit(solution)/shard_map/sjcd,jgfd->sjcgf/dot_general | solution.py:51
  239.5 0.2 fusion.54
  239.6 0.3 maximum_bitcast_fusion.6
  240.0 5.5 %fusion.8 = bf16[64,8,4096]{2,0,1:T(8,128)(2,1)S(1)} fusion(bf16[1,192,4096]{2,1,0:T(8,128)(2,1)} %collective-permute-done.2, bf16[1,192,4096]{2,1,0:T(8,128)(2,1)} %collective-permute-done.1, bf16[1,192,4096]{2,1,0:T(8,128)(2,1)} %collective-permute-done, bf16[1,192,4096]{2,1,0:T(8,128)(2,1)S(1)} %copy-done.7, ...), kind=kOutput, calls=%fused_computation.10 | convolution fusion | flops 3248488448 | bytes 11272192 | tf_op jit(solution)/shard_map/sjcf,jfd->sjcd/dot_general | solution.py:57
  245.5 4.3 %copy.45 = bf16[64,8,4096]{2,1,0:T(8,128)(2,1)} copy(bf16[64,8,4096]{2,0,1:T(8,128)(2,1)S(1)} %fusion.8) | data formatting | bytes 8388608 | tf_op jit(solution)/shard_map/reshape | solution.py:61
  249.7 12.7 %all-to-all-start.1 = ((bf16[64,8,4096]{2,1,0:T(8,128)(2,1)}), bf16[64,8,4096]{2,1,0:T(8,128)(2,1)}, u32[]{:S(2)}, u32[]{:S(2)}) async-start(bf16[64,8,4096]{2,1,0:T(8,128)(2,1)} %copy.45), calls=%async_computation.2 | async-start | bytes 8388608 | tf_op jit(solution)/shard_map/all_to_all | solution.py:60
  262.5 0.3 slice_reduce_fusion.8
  262.8 0.1 subtract_convert_fusion
  263.0 94.0 %all-to-all-done.1 = bf16[64,8,4096]{2,1,0:T(8,128)(2,1)} async-done(((bf16[64,8,4096]{2,1,0:T(8,128)(2,1)}), bf16[64,8,4096]{2,1,0:T(8,128)(2,1)}, u32[]{:S(2)}, u32[]{:S(2)}) %all-to-all-start.1) | async-done | bytes 4194336 | tf_op jit(solution)/shard_map/all_to_all | solution.py:60
  357.0 3.0 fusion.12
  360.0 0.8 fusion.46
  (36 shorter events, 0.7 us)
Async XLA Ops:
  6.5 1.0 copy-start
  6.5 7.0 %copy-start.4 = (s32[32,8]{0,1:T(8,128)S(1)}, s32[32,8]{0,1:T(8,128)}, u32[]{:S(2)}) copy-start(s32[32,8]{0,1:T(8,128)} %param.12) | copy-start | bytes 3076
  6.5 8.3 %copy-start.3 = (bf16[4096]{0:T(1024)(128)(2,1)S(1)}, bf16[4096]{0:T(1024)(128)(2,1)}, u32[]{:S(2)}) copy-start(bf16[4096]{0:T(1024)(128)(2,1)} %param.11) | copy-start | bytes 24580
  6.5 41.9 %copy-start.2 = (bf16[32,4096]{1,0:T(8,128)(2,1)S(1)}, bf16[32,4096]{1,0:T(8,128)(2,1)}, u32[]{:S(2)}) copy-start(bf16[32,4096]{1,0:T(8,128)(2,1)} %param.10) | copy-start | bytes 786436
  6.5 41.9 %reduce-scatter.2.cloned.1.call-start = ((), (), s32[]{:S(2)}) async-start(), calls=%async_computation.3 | async-start | bytes 2621440 | tf_op jit(solution)/shard_map/reduce_scatter | solution.py:26
  54.0 126.7 %copy-start.7 = (bf16[1,192,4096]{2,1,0:T(8,128)(2,1)S(1)}, bf16[1,192,4096]{2,1,0:T(8,128)(2,1)}, u32[]{:S(2)}) copy-start(bf16[1,192,4096]{2,1,0:T(8,128)(2,1)} %param.15) | copy-start | bytes 4718596
  54.0 163.7 %all-to-all-start = ((bf16[64,8,4096]{2,1,0:T(8,128)(2,1)}), bf16[64,8,4096]{2,1,0:T(8,128)(2,1)}, u32[]{:S(2)}, u32[]{:S(2)}) async-start(bf16[64,8,4096]{2,1,0:T(8,128)(2,1)} %fusion.9), calls=%async_computation.1 | async-start | bytes 8388608 | tf_op jit(solution)/shard_map/all_to_all | solution.py:47
  66.8 112.9 %collective-permute-start.3 = (bf16[1,2,192,4096]{3,2,1,0:T(8,128)(2,1)}, bf16[1,2,192,4096]{3,2,1,0:T(8,128)(2,1)}, u32[]{:S(2)}, u32[]{:S(2)}) collective-permute-start(bf16[1,2,192,4096]{3,2,1,0:T(8,128)(2,1)} %param.14), channel_id=1, source_target_pairs={{0,2},{1,3},{2,0},{3,1},{4,6},{5,7},{6,4},{7,5},{8,10},{9,11},{10,... | collective-permute-start | bytes 9437192 | tf_op jit(solution)/shard_map/ppermute | solution.py:13
  179.7 43.5 %collective-permute-start.5 = (bf16[1,2,192,4096]{3,2,1,0:T(8,128)(2,1)}, bf16[1,2,192,4096]{3,2,1,0:T(8,128)(2,1)}, u32[]{:S(2)}, u32[]{:S(2)}) collective-permute-start(bf16[1,2,192,4096]{3,2,1,0:T(8,128)(2,1)} %collective-permute-done.3), channel_id=1, source_target_pairs={{0,1},{1,0},{2,3},{3,2},{4,5},{5,4},{6,7},{7,6},{8,9},{9,8},{10,11... | collective-permute-start | bytes 9437192 | tf_op jit(solution)/shard_map/ppermute | solution.py:14
  180.8 48.0 %collective-permute-start.4 = (bf16[1,2,192,4096]{3,2,1,0:T(8,128)(2,1)}, bf16[1,2,192,4096]{3,2,1,0:T(8,128)(2,1)}, u32[]{:S(2)}, u32[]{:S(2)}) collective-permute-start(bf16[1,2,192,4096]{3,2,1,0:T(8,128)(2,1)} %param.14), channel_id=1, source_target_pairs={{0,1},{1,0},{2,3},{3,2},{4,5},{5,4},{6,7},{7,6},{8,9},{9,8},{10,11... | collective-permute-start | bytes 9437192 | tf_op jit(solution)/shard_map/ppermute | solution.py:14
  180.8 35.5 %collective-permute-start = (bf16[1,192,4096]{2,1,0:T(8,128)(2,1)S(1)}, bf16[1,192,4096]{2,1,0:T(8,128)(2,1)}, u32[]{:S(2)}, u32[]{:S(2)}) collective-permute-start(bf16[1,192,4096]{2,1,0:T(8,128)(2,1)S(1)} %copy-done.7), channel_id=1, source_target_pairs={{0,2},{1,3},{2,0},{3,1},{4,6},{5,7},{6,4},{7,5},{8,10},{9,11},{10,... | collective-permute-start | bytes 4718600 | tf_op jit(solution)/shard_map/ppermute | solution.py:13
  182.2 57.8 %collective-permute-start.1 = (bf16[1,192,4096]{2,1,0:T(8,128)(2,1)S(1)}, bf16[1,192,4096]{2,1,0:T(8,128)(2,1)}, u32[]{:S(2)}, u32[]{:S(2)}) collective-permute-start(bf16[1,192,4096]{2,1,0:T(8,128)(2,1)S(1)} %copy-done.7), channel_id=1, source_target_pairs={{0,1},{1,0},{2,3},{3,2},{4,5},{5,4},{6,7},{7,6},{8,9},{9,8},{10,11... | collective-permute-start | bytes 4718600 | tf_op jit(solution)/shard_map/ppermute | solution.py:14
  216.3 23.6 %collective-permute-start.2 = (bf16[1,192,4096]{2,1,0:T(8,128)(2,1)}, bf16[1,192,4096]{2,1,0:T(8,128)(2,1)}, u32[]{:S(2)}, u32[]{:S(2)}) collective-permute-start(bf16[1,192,4096]{2,1,0:T(8,128)(2,1)} %collective-permute-done), channel_id=1, source_target_pairs={{0,1},{1,0},{2,3},{3,2},{4,5},{5,4},{6,7},{7,6},{8,9},{9,8},{10,11... | collective-permute-start | bytes 4718600 | tf_op jit(solution)/shard_map/ppermute | solution.py:14
  228.8 6.2 %copy-start.6 = (bf16[1,2,192,4096]{3,2,1,0:T(8,128)(2,1)S(1)}, bf16[1,2,192,4096]{3,2,1,0:T(8,128)(2,1)}, u32[]{:S(2)}) copy-start(bf16[1,2,192,4096]{3,2,1,0:T(8,128)(2,1)} %param.14) | copy-start | bytes 9437188
  249.7 13.1 %copy-start.5 = (f32[32,8]{0,1:T(8,128)S(1)}, f32[32,8]{0,1:T(8,128)}, u32[]{:S(2)}) copy-start(f32[32,8]{0,1:T(8,128)} %param.13) | copy-start | bytes 3076
  249.7 107.2 %all-to-all-start.1 = ((bf16[64,8,4096]{2,1,0:T(8,128)(2,1)}), bf16[64,8,4096]{2,1,0:T(8,128)(2,1)}, u32[]{:S(2)}, u32[]{:S(2)}) async-start(bf16[64,8,4096]{2,1,0:T(8,128)(2,1)} %copy.45), calls=%async_computation.2 | async-start | bytes 8388608 | tf_op jit(solution)/shard_map/all_to_all | solution.py:60
  262.5 97.5 %copy-start.1 = (f32[32,4096]{1,0:T(8,128)S(1)}, f32[32,4096]{1,0:T(8,128)}, u32[]{:S(2)}) copy-start(f32[32,4096]{1,0:T(8,128)} %reduce-scatter.2.cloned.1.call-done) | copy-start | bytes 1572868
Sparse Core Ops, SparseCore 0:
  13.6 34.8 reduce-scatter.1

commit v3 on v2

--- a/solution.py
+++ b/solution.py
@@ -15,7 +15,7 @@
     return [own, far, near_own, near_far]
 
 
-def local(context, wo_proj, residual, norm_gain, expert_ids, route_weights, w_gate_up, w_down):
+def layer(context, wo_proj, residual, norm_gain, expert_ids, route_weights, w_gate_up, w_down):
     quarter_rows, model_width = residual.shape
     top_count = expert_ids.shape[1]
     exp_local = w_gate_up.shape[0]
@@ -23,8 +23,9 @@
     experts = exp_local * ep_size
     capacity = max(2, min(quarter_rows, 2 * quarter_rows * top_count // experts))
     pieces = gather_weights(w_gate_up, w_down)
+    attn_part = jnp.dot(context, wo_proj, preferred_element_type=jnp.float32)
     attn = lax.psum_scatter(
-        jnp.dot(context, wo_proj, preferred_element_type=jnp.float32),
+        attn_part,
         "tp",
         scatter_dimension=0,
         tiled=True,
@@ -46,16 +47,17 @@
     send_rows = send_rows.reshape(ep_size, exp_local * capacity, model_width)
     received = lax.all_to_all(send_rows, "ep", split_axis=0, concat_axis=0, tiled=True)
     received = received.reshape(ep_size, exp_local, capacity, model_width)
-    activated = []
-    for gate_up_piece, _ in pieces:
-        both = jnp.einsum(
-            "sjcd,jgfd->sjcgf", received, gate_up_piece, preferred_element_type=jnp.float32
-        )
-        activated.append((jax.nn.silu(both[:, :, :, 0]) * both[:, :, :, 1]).astype(jnp.bfloat16))
-    activated = jnp.concatenate(activated, axis=3)
-    down_full = jnp.concatenate([down_piece for _, down_piece in pieces], axis=1)
-    expert_out = jnp.einsum(
-        "sjcf,jfd->sjcd", activated, down_full, preferred_element_type=jnp.float32
+    slots = ep_size * exp_local * capacity
+    rows = received.reshape(slots, model_width)
+    gate_up_full = jnp.concatenate(
+        [piece.reshape(-1, model_width) for piece, _ in pieces], axis=0
+    )
+    down_full = jnp.concatenate([piece.reshape(-1, model_width) for _, piece in pieces], axis=0)
+    both = jnp.dot(rows, gate_up_full.T, preferred_element_type=jnp.float32)
+    both = both.reshape(slots, len(pieces), 2, -1)
+    activated = (jax.nn.silu(both[:, :, 0]) * both[:, :, 1]).astype(jnp.bfloat16)
+    expert_out = jnp.dot(
+        activated.reshape(slots, -1), down_full, preferred_element_type=jnp.float32
     ).astype(jnp.bfloat16)
     returned = lax.all_to_all(
         expert_out.reshape(ep_size, exp_local * capacity, model_width),
@@ -91,4 +93,4 @@
         P("ep", "tp", None),
     )
     out_specs = P(("ep", "tp"), None)
-    return jax.shard_map(local, mesh=mesh, in_specs=in_specs, out_specs=out_specs, check_vma=False)
+    return jax.shard_map(layer, mesh=mesh, in_specs=in_specs, out_specs=out_specs, check_vma=False)

time: 370 us -> 385 us (1.041)
  other arithmetic: 4.16 us -> 32.4 us
  matrix products: 40.1 us -> 30.6 us
    concatenate x0 -> x1, other arithmetic: none -> 28.7 us  [layer(): jnp.concatenate([piece.reshape(-1, model_width) for piece, _ in pieces],...]
    dot_general x8 -> x5, matrix products: 40.1 us -> 30.6 us  [the longest x1 10.6 us: layer(): both = jnp.dot(rows, gate_up_full.T, preferred_element_type=jnp.float32)]
    reshape x1 -> x0, local copies, waits for them, and re-layouts: 4.27 us -> none  [local(): expert_out.reshape(ep_size, exp_local * capacity, model_width)]
  transfers between devices with their start and end apart: 9 -> 9, of which waited for: 4 -> 4; matrix products, arithmetic and copies ran while one was open for 7% -> 11% of each run, Pallas kernels for 0% -> 0%
where the time goes in v3:
time: 385 us; the launch traced here: 383 us
  waiting for transfers between devices  274 us (71%)
  other arithmetic  32.4 us (8%)
  matrix products  30.6 us (8%)
  starting transfers between devices  30.1 us (8%)
  between operations  13.6 us (4%)
    ppermute x2, waiting for transfers between devices, gather_weights(): far = lax.ppermute(own, 'tp', far_pairs)  146 us
    all_to_all x1, waiting for transfers between devices, layer(): lax.all_to_all(expert_out.reshape(ep_size, exp_local * capacity, model_wi...  93.8 us
    reduce_scatter x1, waiting for transfers between devices, layer(): attn = lax.psum_scatter(attn_part, 'tp', scatter_dimension=0, tiled=True)  33.4 us
    concatenate x1, other arithmetic, layer(): jnp.concatenate([piece.reshape(-1, model_width) for piece, _ in pieces],...  28.7 us
    all_to_all x1, starting transfers between devices, layer(): lax.all_to_all(send_rows, 'ep', split_axis=0, concat_axis=0, tiled=True)  12.9 us
    all_to_all x1, starting transfers between devices, layer(): lax.all_to_all(expert_out.reshape(ep_size, exp_local * capacity, model_wi...  12.7 us
    dot_general x1, matrix products, layer(): both = jnp.dot(rows, gate_up_full.T, preferred_element_type=jnp.float32)  10.6 us
  transfers between devices with their start and end apart: 9, of which 4 were waited for; matrix products, arithmetic and copies ran while one was open for 11% of the time, Pallas kernels for 0%

profile of v3, /device:TPU:1, one launch (start us, length us, event | category | flops | bytes accessed | tf_op | source)
XLA Modules:
  0.0 383.1 jit_solution(4409103293568106014)
XLA Ops:
  6.6 0.9 copy-done
  7.5 6.0 %fusion.40 = f32[128,4096]{1,0:T(8,128)} fusion(bf16[128,1024]{1,0:T(8,128)(2,1)S(1)} %copy-done, bf16[1024,4096]{1,0:T(8,128)(2,1)} %param.9), kind=kOutput, calls=%fused_computation.78 | convolution fusion | flops 1073741824 | bytes 10747904 | tf_op jit(solution)/shard_map/dot_general | solution.py:26
  13.6 0.1 eq.160
  13.7 0.1 eq.164
  13.8 0.6 reduce-window.6
  14.4 0.2 slice_reduce_fusion
  14.6 0.1 fusion.30
  14.9 0.2 fusion.25
  15.1 33.4 %reduce-scatter.2.cloned.1.call-done = f32[32,4096]{1,0:T(8,128)} async-done(((f32[128,4096]{1,0:T(8,128)}), f32[32,4096]{1,0:T(8,128)}) %reduce-scatter.2.cloned.1.call-update) | async-done | bytes 524304 | tf_op jit(solution)/shard_map/reduce_scatter | solution.py:27
  48.5 1.2 multiply_reduce_fusion
  49.7 4.3 %fusion.11 = bf16[64,8,4096]{2,1,0:T(8,128)(2,1)} fusion(pred[512,32]{0,1:T(8,128)(4,1)S(1)} %fusion.25, f32[4096]{0:T(1024)S(1)} %convert_element_type.45, f32[32]{0:T(128)S(1)} %add_rsqrt_fusion, f32[32,4096]{1,0:T(8,128)} %reduce-scatter.2.cloned.1.call-done, bf16[32,4096]{1,0:T(8,128)(2,1)S(1)} %copy-done.4), kind=kOutput, calls=%fused_computation.11 | convolution fusion | flops 136970240 | bytes 5013632 | tf_op jit(solution)/shard_map/dot_general | solution.py:46
  54.0 12.9 %all-to-all-start = ((bf16[64,8,4096]{2,1,0:T(8,128)(2,1)}), bf16[64,8,4096]{2,1,0:T(8,128)(2,1)}, u32[]{:S(2)}, u32[]{:S(2)}) async-start(bf16[64,8,4096]{2,1,0:T(8,128)(2,1)} %fusion.11), calls=%async_computation.1 | async-start | bytes 8388608 | tf_op jit(solution)/shard_map/all_to_all | solution.py:48
  66.9 0.1 collective-permute-start
  67.0 0.8 collective-permute-start.1
  67.8 111.9 %collective-permute-done = bf16[1,2,192,4096]{3,2,1,0:T(8,128)(2,1)S(1)} collective-permute-done((bf16[1,2,192,4096]{3,2,1,0:T(8,128)(2,1)S(1)}, bf16[1,2,192,4096]{3,2,1,0:T(8,128)(2,1)S(1)}, u32[]{:S(2)}, u32[]{:S(2)}) %collective-permute-start) | collective-permute-done | bytes 3145760 | tf_op jit(solution)/shard_map/ppermute | solution.py:13
  179.7 1.0 collective-permute-start.2
  180.8 1.4 collective-permute-start.3
  182.2 0.3 collective-permute-start.4
  182.5 34.6 %collective-permute-done.3 = bf16[1,192,4096]{2,1,0:T(8,128)(2,1)} collective-permute-done((bf16[1,192,4096]{2,1,0:T(8,128)(2,1)}, bf16[1,192,4096]{2,1,0:T(8,128)(2,1)}, u32[]{:S(2)}, u32[]{:S(2)}) %collective-permute-start.3) | collective-permute-done | bytes 1572896 | tf_op jit(solution)/shard_map/ppermute | solution.py:13
  217.0 0.9 collective-permute-start.5
  217.9 28.7 %pad_maximum_fusion = bf16[1536,4096]{1,0:T(8,128)(2,1)} fusion(bf16[384,4096]{1,0:T(8,128)(2,1)S(1)} %bitcast.84, bf16[384,4096]{1,0:T(8,128)(2,1)S(1)} %bitcast.83, bf16[384,4096]{1,0:T(8,128)(2,1)S(1)} %bitcast.82, bf16[384,4096]{1,0:T(8,128)(2,1)S(1)} %bitcast.81), kind=kLoop, calls=%fused_computation | loop fusion | flops 50331648 | bytes 25165824 | tf_op jit(solution)/shard_map/concatenate | solution.py:52
  246.6 10.6 %fusion.15 = f32[512,4,2,192]{0,3,2,1:T(8,128)S(1)} fusion(bf16[4,2,192,4096]{3,2,1,0:T(8,128)(2,1)} %bitcast.80, bf16[64,8,4096]{2,1,0:T(8,128)(2,1)} %all-to-all-done), kind=kOutput, calls=%fused_computation.13 | convolution fusion | flops 6442450944 | bytes 19922944 | tf_op jit(solution)/shard_map/dot_general | solution.py:56
  257.2 0.5 fusion.39
  257.7 0.5 fusion.19
  258.2 0.3 copy-done.9
  258.6 6.7 %fusion.12 = bf16[64,8,4096]{2,1,0:T(8,128)(2,1)} fusion(bf16[512,768]{0,1:T(8,128)(2,1)S(1)} %fusion.19, bf16[192,4096]{1,0:T(8,128)(2,1)} %bitcast.23, bf16[192,4096]{1,0:T(8,128)(2,1)} %bitcast.22, bf16[192,4096]{1,0:T(8,128)(2,1)} %bitcast.21, bf16[192,4096]{1,0:T(8,128)(2,1)S(1)} %bitcast.85), kind=kOutput, calls=%fused_computation.12 | convolution fusion | flops 3248488448 | bytes 11272192 | tf_op jit(solution)/shard_map/dot_general | solution.py:59
  265.3 12.7 %all-to-all-start.1 = ((bf16[64,8,4096]{2,1,0:T(8,128)(2,1)}), bf16[64,8,4096]{2,1,0:T(8,128)(2,1)}, u32[]{:S(2)}, u32[]{:S(2)}) async-start(bf16[64,8,4096]{2,1,0:T(8,128)(2,1)} %fusion.12), calls=%async_computation.2 | async-start | bytes 8388608 | tf_op jit(solution)/shard_map/all_to_all | solution.py:62
  278.0 0.3 slice_reduce_fusion.8
  278.4 0.1 subtract_convert_fusion
  278.5 93.8 %all-to-all-done.1 = bf16[64,8,4096]{2,1,0:T(8,128)(2,1)} async-done(((bf16[64,8,4096]{2,1,0:T(8,128)(2,1)}), bf16[64,8,4096]{2,1,0:T(8,128)(2,1)}, u32[]{:S(2)}, u32[]{:S(2)}) %all-to-all-start.1) | async-done | bytes 4194336 | tf_op jit(solution)/shard_map/all_to_all | solution.py:62
  372.3 3.0 fusion.17
  375.4 0.8 fusion.24
  (34 shorter events, 0.3 us)
Async XLA Ops:
  6.5 1.0 copy-start
  6.5 7.0 %copy-start.7 = (s32[32,8]{0,1:T(8,128)S(1)}, s32[32,8]{0,1:T(8,128)}, u32[]{:S(2)}) copy-start(s32[32,8]{0,1:T(8,128)} %param.12) | copy-start | bytes 3076
  6.5 8.3 %copy-start.6 = (bf16[4096]{0:T(1024)(128)(2,1)S(1)}, bf16[4096]{0:T(1024)(128)(2,1)}, u32[]{:S(2)}) copy-start(bf16[4096]{0:T(1024)(128)(2,1)} %param.11) | copy-start | bytes 24580
  6.5 41.9 %copy-start.4 = (bf16[32,4096]{1,0:T(8,128)(2,1)S(1)}, bf16[32,4096]{1,0:T(8,128)(2,1)}, u32[]{:S(2)}) copy-start(bf16[32,4096]{1,0:T(8,128)(2,1)} %param.10) | copy-start | bytes 786436
  6.5 41.9 %reduce-scatter.2.cloned.1.call-start = ((), (), s32[]{:S(2)}) async-start(), calls=%async_computation.3 | async-start | bytes 2621440 | tf_op jit(solution)/shard_map/reduce_scatter | solution.py:27
  54.0 12.9 %copy-start.3 = (bf16[1,2,192,4096]{3,2,1,0:T(8,128)(2,1)S(1)}, bf16[1,2,192,4096]{3,2,1,0:T(8,128)(2,1)}, u32[]{:S(2)}) copy-start(bf16[1,2,192,4096]{3,2,1,0:T(8,128)(2,1)} %param.14) | copy-start | bytes 9437188
  54.0 192.6 %all-to-all-start = ((bf16[64,8,4096]{2,1,0:T(8,128)(2,1)}), bf16[64,8,4096]{2,1,0:T(8,128)(2,1)}, u32[]{:S(2)}, u32[]{:S(2)}) async-start(bf16[64,8,4096]{2,1,0:T(8,128)(2,1)} %fusion.11), calls=%async_computation.1 | async-start | bytes 8388608 | tf_op jit(solution)/shard_map/all_to_all | solution.py:48
  66.9 112.9 %collective-permute-start = (bf16[1,2,192,4096]{3,2,1,0:T(8,128)(2,1)S(1)}, bf16[1,2,192,4096]{3,2,1,0:T(8,128)(2,1)S(1)}, u32[]{:S(2)}, u32[]{:S(2)}) collective-permute-start(bf16[1,2,192,4096]{3,2,1,0:T(8,128)(2,1)S(1)} %copy-done.3), channel_id=1, source_target_pairs={{0,2},{1,3},{2,0},{3,1},{4,6},{5,7},{6,4},{7,5},{8,10},{9,11},{10,... | collective-permute-start | bytes 9437192 | tf_op jit(solution)/shard_map/ppermute | solution.py:13
  67.0 150.9 %collective-permute-start.1 = (bf16[1,2,192,4096]{3,2,1,0:T(8,128)(2,1)S(1)}, bf16[1,2,192,4096]{3,2,1,0:T(8,128)(2,1)S(1)}, u32[]{:S(2)}, u32[]{:S(2)}) collective-permute-start(bf16[1,2,192,4096]{3,2,1,0:T(8,128)(2,1)S(1)} %copy-done.3), channel_id=1, source_target_pairs={{0,1},{1,0},{2,3},{3,2},{4,5},{5,4},{6,7},{7,6},{8,9},{9,8},{10,11... | collective-permute-start | bytes 9437192 | tf_op jit(solution)/shard_map/ppermute | solution.py:14
  179.7 38.2 %collective-permute-start.2 = (bf16[1,2,192,4096]{3,2,1,0:T(8,128)(2,1)S(1)}, bf16[1,2,192,4096]{3,2,1,0:T(8,128)(2,1)S(1)}, u32[]{:S(2)}, u32[]{:S(2)}) collective-permute-start(bf16[1,2,192,4096]{3,2,1,0:T(8,128)(2,1)S(1)} %collective-permute-done), channel_id=1, source_target_pairs={{0,1},{1,0},{2,3},{3,2},{4,5},{5,4},{6,7},{7,6},{8,9},{9,8},{10,11... | collective-permute-start | bytes 9437192 | tf_op jit(solution)/shard_map/ppermute | solution.py:14
  180.8 36.3 %collective-permute-start.3 = (bf16[1,192,4096]{2,1,0:T(8,128)(2,1)}, bf16[1,192,4096]{2,1,0:T(8,128)(2,1)}, u32[]{:S(2)}, u32[]{:S(2)}) collective-permute-start(bf16[1,192,4096]{2,1,0:T(8,128)(2,1)} %param.15), channel_id=1, source_target_pairs={{0,2},{1,3},{2,0},{3,1},{4,6},{5,7},{6,4},{7,5},{8,10},{9,11},{10,... | collective-permute-start | bytes 4718600 | tf_op jit(solution)/shard_map/ppermute | solution.py:13
  182.2 76.0 %collective-permute-start.4 = (bf16[1,192,4096]{2,1,0:T(8,128)(2,1)}, bf16[1,192,4096]{2,1,0:T(8,128)(2,1)}, u32[]{:S(2)}, u32[]{:S(2)}) collective-permute-start(bf16[1,192,4096]{2,1,0:T(8,128)(2,1)} %param.15), channel_id=1, source_target_pairs={{0,1},{1,0},{2,3},{3,2},{4,5},{5,4},{6,7},{7,6},{8,9},{9,8},{10,11... | collective-permute-start | bytes 4718600 | tf_op jit(solution)/shard_map/ppermute | solution.py:14
  217.0 41.2 %collective-permute-start.5 = (bf16[1,192,4096]{2,1,0:T(8,128)(2,1)}, bf16[1,192,4096]{2,1,0:T(8,128)(2,1)}, u32[]{:S(2)}, u32[]{:S(2)}) collective-permute-start(bf16[1,192,4096]{2,1,0:T(8,128)(2,1)} %collective-permute-done.3), channel_id=1, source_target_pairs={{0,1},{1,0},{2,3},{3,2},{4,5},{5,4},{6,7},{7,6},{8,9},{9,8},{10,11... | collective-permute-start | bytes 4718600 | tf_op jit(solution)/shard_map/ppermute | solution.py:14
  257.2 1.4 copy-start.9
  265.3 13.1 %copy-start.8 = (f32[32,8]{0,1:T(8,128)S(1)}, f32[32,8]{0,1:T(8,128)}, u32[]{:S(2)}) copy-start(f32[32,8]{0,1:T(8,128)} %param.13) | copy-start | bytes 3076
  265.3 107.1 %all-to-all-start.1 = ((bf16[64,8,4096]{2,1,0:T(8,128)(2,1)}), bf16[64,8,4096]{2,1,0:T(8,128)(2,1)}, u32[]{:S(2)}, u32[]{:S(2)}) async-start(bf16[64,8,4096]{2,1,0:T(8,128)(2,1)} %fusion.12), calls=%async_computation.2 | async-start | bytes 8388608 | tf_op jit(solution)/shard_map/all_to_all | solution.py:62
  278.0 97.4 %copy-start.2 = (f32[32,4096]{1,0:T(8,128)S(1)}, f32[32,4096]{1,0:T(8,128)}, u32[]{:S(2)}) copy-start(f32[32,4096]{1,0:T(8,128)} %reduce-scatter.2.cloned.1.call-done) | copy-start | bytes 1572868
  278.0 97.4 %copy-start.5 = (bf16[32,4096]{1,0:T(8,128)(2,1)S(1)}, bf16[32,4096]{1,0:T(8,128)(2,1)}, u32[]{:S(2)}) copy-start(bf16[32,4096]{1,0:T(8,128)(2,1)} %param.10) | copy-start | bytes 786436
  278.0 98.2 %copy-start.1 = (bf16[128,1024]{1,0:T(8,128)(2,1)S(1)}, bf16[128,1024]{1,0:T(8,128)(2,1)}, u32[]{:S(2)}) copy-start(bf16[128,1024]{1,0:T(8,128)(2,1)} %param.8) | copy-start | bytes 786436
Sparse Core Ops, SparseCore 0:
  13.6 34.8 reduce-scatter.1

commit v4 on v3

--- a/solution.py
+++ b/solution.py
@@ -24,12 +24,10 @@
     capacity = max(2, min(quarter_rows, 2 * quarter_rows * top_count // experts))
     pieces = gather_weights(w_gate_up, w_down)
     attn_part = jnp.dot(context, wo_proj, preferred_element_type=jnp.float32)
-    attn = lax.psum_scatter(
-        attn_part,
-        "tp",
-        scatter_dimension=0,
-        tiled=True,
-    )
+    tp_size = lax.axis_size("tp")
+    shares = attn_part.astype(jnp.bfloat16).reshape(tp_size, quarter_rows, model_width)
+    shares = lax.all_to_all(shares, "tp", split_axis=0, concat_axis=0, tiled=True)
+    attn = jnp.sum(shares.astype(jnp.float32), axis=0)
     hidden = residual.astype(jnp.float32) + attn
     inverse_rms = lax.rsqrt(jnp.mean(hidden * hidden, axis=1, keepdims=True) + 1e-06)
     normed = (hidden * inverse_rms * norm_gain.astype(jnp.float32)).astype(jnp.bfloat16)

time: 385 us -> 334 us (0.87)
  waiting for transfers between devices: 274 us -> 252 us
  other arithmetic: 32.4 us -> 11.1 us
  between operations: 13.6 us -> 0.18 us
  starting transfers between devices: 30.1 us -> 36.8 us
    reduce_scatter x1 -> x0, waiting for transfers between devices: 33.4 us -> none  [layer(): attn = lax.psum_scatter(attn_part, 'tp', scatter_dimension=0, tiled=True)]
    concatenate x1, other arithmetic: 28.7 us -> 8.23 us  [layer(): jnp.concatenate([piece.reshape(-1, model_width) for piece, _ in pieces],...]
    all_to_all x0 -> x1, waiting for transfers between devices: none -> 11.9 us  [layer(): lax.all_to_all(shares, 'tp', split_axis=0, concat_axis=0, tiled=True)]
    all_to_all x0 -> x1, starting transfers between devices: none -> 6.81 us  [layer(): lax.all_to_all(shares, 'tp', split_axis=0, concat_axis=0, tiled=True)]
  transfers between devices with their start and end apart: 9 -> 9, of which waited for: 4 -> 4; matrix products, arithmetic and copies ran while one was open for 11% -> 7% of each run, Pallas kernels for 0% -> 0%
where the time goes in v4:
time: 334 us; the launch traced here: 332 us
  waiting for transfers between devices  252 us (75%)
  starting transfers between devices  36.8 us (11%)
  matrix products  29.2 us (9%)
  other arithmetic  11.1 us (3%)
    ppermute x2, waiting for transfers between devices, gather_weights(): far = lax.ppermute(own, 'tp', far_pairs)  147 us
    all_to_all x1, waiting for transfers between devices, layer(): lax.all_to_all(expert_out.reshape(ep_size, exp_local * capacity, model_wi...  94 us
    all_to_all x1, starting transfers between devices, layer(): lax.all_to_all(send_rows, 'ep', split_axis=0, concat_axis=0, tiled=True)  12.8 us
    all_to_all x1, starting transfers between devices, layer(): lax.all_to_all(expert_out.reshape(ep_size, exp_local * capacity, model_wi...  12.5 us
    all_to_all x1, waiting for transfers between devices, layer(): lax.all_to_all(shares, 'tp', split_axis=0, concat_axis=0, tiled=True)  11.9 us
    dot_general x1, matrix products, layer(): both = jnp.dot(rows, gate_up_full.T, preferred_element_type=jnp.float32)  10.6 us
    concatenate x1, other arithmetic, layer(): jnp.concatenate([piece.reshape(-1, model_width) for piece, _ in pieces],...  8.23 us
    all_to_all x1, starting transfers between devices, layer(): lax.all_to_all(shares, 'tp', split_axis=0, concat_axis=0, tiled=True)  6.81 us
  transfers between devices with their start and end apart: 9, of which 4 were waited for; matrix products, arithmetic and copies ran while one was open for 7% of the time, Pallas kernels for 0%

profile of v4, /device:TPU:1, one launch (start us, length us, event | category | flops | bytes accessed | tf_op | source)
XLA Modules:
  0.0 332.3 jit_solution(5585574362751187200)
XLA Ops:
  0.0 0.9 copy-done
  1.0 5.6 %convolution_convert_fusion.1 = bf16[128,4096]{1,0:T(8,128)(2,1)} fusion(bf16[128,1024]{1,0:T(8,128)(2,1)S(1)} %copy-done, bf16[1024,4096]{1,0:T(8,128)(2,1)} %param.9), kind=kOutput, calls=%fused_computation.13 | convolution fusion | flops 1074266112 | bytes 9699328 | tf_op jit(solution)/shard_map/dot_general | solution.py:26
  6.6 6.8 %all-to-all-start = ((bf16[4,32,4096]{2,1,0:T(8,128)(2,1)}), bf16[4,32,4096]{2,1,0:T(8,128)(2,1)S(1)}, u32[]{:S(2)}, u32[]{:S(2)}) async-start(bf16[4,32,4096]{2,1,0:T(8,128)(2,1)} %bitcast), calls=%async_computation | async-start | bytes 2097152 | tf_op jit(solution)/shard_map/all_to_all | solution.py:29
  13.7 0.6 reduce-window.6
  14.3 0.2 slice_reduce_fusion
  14.5 0.1 fusion.30
  14.8 0.2 fusion.25
  15.0 11.9 %all-to-all-done = bf16[4,32,4096]{2,1,0:T(8,128)(2,1)S(1)} async-done(((bf16[4,32,4096]{2,1,0:T(8,128)(2,1)}), bf16[4,32,4096]{2,1,0:T(8,128)(2,1)S(1)}, u32[]{:S(2)}, u32[]{:S(2)}) %all-to-all-start) | async-done | bytes 1048608 | tf_op jit(solution)/shard_map/all_to_all | solution.py:29
  26.9 0.2 convert_reduce_fusion
  27.0 0.2 multiply_reduce_fusion
  27.2 3.2 fusion.11
  30.5 12.8 %all-to-all-start.1 = ((bf16[64,8,4096]{2,1,0:T(8,128)(2,1)}), bf16[64,8,4096]{2,1,0:T(8,128)(2,1)}, u32[]{:S(2)}, u32[]{:S(2)}) async-start(bf16[64,8,4096]{2,1,0:T(8,128)(2,1)} %fusion.11), calls=%async_computation.1 | async-start | bytes 8388608 | tf_op jit(solution)/shard_map/all_to_all | solution.py:46
  43.3 0.1 collective-permute-start
  43.4 1.3 collective-permute-start.1
  44.8 111.8 %collective-permute-done = bf16[1,2,192,4096]{3,2,1,0:T(8,128)(2,1)S(1)} collective-permute-done((bf16[1,2,192,4096]{3,2,1,0:T(8,128)(2,1)}, bf16[1,2,192,4096]{3,2,1,0:T(8,128)(2,1)S(1)}, u32[]{:S(2)}, u32[]{:S(2)}) %collective-permute-start) | collective-permute-done | bytes 3145760 | tf_op jit(solution)/shard_map/ppermute | solution.py:13
  156.6 0.8 collective-permute-start.2
  157.4 1.2 collective-permute-start.3
  158.7 0.3 collective-permute-start.4
  158.9 34.7 %collective-permute-done.3 = bf16[1,192,4096]{2,1,0:T(8,128)(2,1)} collective-permute-done((bf16[1,192,4096]{2,1,0:T(8,128)(2,1)}, bf16[1,192,4096]{2,1,0:T(8,128)(2,1)}, u32[]{:S(2)}, u32[]{:S(2)}) %collective-permute-start.3) | collective-permute-done | bytes 1572896 | tf_op jit(solution)/shard_map/ppermute | solution.py:13
  193.7 0.9 collective-permute-start.5
  194.6 8.2 %pad_maximum_fusion = bf16[1536,4096]{1,0:T(8,128)(2,1)} fusion(bf16[384,4096]{1,0:T(8,128)(2,1)S(1)} %bitcast.85, bf16[384,4096]{1,0:T(8,128)(2,1)S(1)} %bitcast.84, bf16[384,4096]{1,0:T(8,128)(2,1)S(1)} %bitcast.83, bf16[384,4096]{1,0:T(8,128)(2,1)} %bitcast.82), kind=kLoop, calls=%fused_computation | loop fusion | flops 50331648 | bytes 25165824 | tf_op jit(solution)/shard_map/concatenate | solution.py:50
  202.8 10.6 %fusion.15 = f32[512,4,2,192]{0,3,2,1:T(8,128)S(1)} fusion(bf16[4,2,192,4096]{3,2,1,0:T(8,128)(2,1)} %bitcast.81, bf16[64,8,4096]{2,1,0:T(8,128)(2,1)} %all-to-all-done.1), kind=kOutput, calls=%fused_computation.14 | convolution fusion | flops 6442450944 | bytes 19922944 | tf_op jit(solution)/shard_map/dot_general | solution.py:54
  213.4 0.5 fusion.39
  213.9 0.5 fusion.19
  214.5 0.3 copy-done.6
  214.8 6.7 %fusion.12 = bf16[64,8,4096]{2,1,0:T(8,128)(2,1)} fusion(bf16[512,768]{0,1:T(8,128)(2,1)S(1)} %fusion.19, bf16[192,4096]{1,0:T(8,128)(2,1)} %bitcast.24, bf16[192,4096]{1,0:T(8,128)(2,1)} %bitcast.23, bf16[192,4096]{1,0:T(8,128)(2,1)} %bitcast.22, bf16[192,4096]{1,0:T(8,128)(2,1)S(1)} %bitcast.86), kind=kOutput, calls=%fused_computation.12 | convolution fusion | flops 3248488448 | bytes 11272192 | tf_op jit(solution)/shard_map/dot_general | solution.py:57
  221.5 12.5 %all-to-all-start.2 = ((bf16[64,8,4096]{2,1,0:T(8,128)(2,1)}), bf16[64,8,4096]{2,1,0:T(8,128)(2,1)}, u32[]{:S(2)}, u32[]{:S(2)}) async-start(bf16[64,8,4096]{2,1,0:T(8,128)(2,1)} %fusion.12), calls=%async_computation.2 | async-start | bytes 8388608 | tf_op jit(solution)/shard_map/all_to_all | solution.py:60
  234.0 0.3 slice_reduce_fusion.8
  234.3 0.1 subtract_convert_fusion
  234.4 94.0 %all-to-all-done.2 = bf16[64,8,4096]{2,1,0:T(8,128)(2,1)} async-done(((bf16[64,8,4096]{2,1,0:T(8,128)(2,1)}), bf16[64,8,4096]{2,1,0:T(8,128)(2,1)}, u32[]{:S(2)}, u32[]{:S(2)}) %all-to-all-start.2) | async-done | bytes 4194336 | tf_op jit(solution)/shard_map/all_to_all | solution.py:60
  328.4 3.0 fusion.17
  331.5 0.8 fusion.24
  (28 shorter events, 0.5 us)
Async XLA Ops:
  0.0 1.0 copy-start
  0.0 13.4 %copy-start.4 = (s32[32,8]{0,1:T(8,128)S(1)}, s32[32,8]{0,1:T(8,128)}, u32[]{:S(2)}) copy-start(s32[32,8]{0,1:T(8,128)} %param.12) | copy-start | bytes 3076
  0.0 14.7 %copy-start.3 = (bf16[4096]{0:T(1024)(128)(2,1)S(1)}, bf16[4096]{0:T(1024)(128)(2,1)}, u32[]{:S(2)}) copy-start(bf16[4096]{0:T(1024)(128)(2,1)} %param.11) | copy-start | bytes 24580
  6.6 20.4 %copy-start.2 = (bf16[32,4096]{1,0:T(8,128)(2,1)S(1)}, bf16[32,4096]{1,0:T(8,128)(2,1)}, u32[]{:S(2)}) copy-start(bf16[32,4096]{1,0:T(8,128)(2,1)} %param.10) | copy-start | bytes 786436
  6.6 20.3 %all-to-all-start = ((bf16[4,32,4096]{2,1,0:T(8,128)(2,1)}), bf16[4,32,4096]{2,1,0:T(8,128)(2,1)S(1)}, u32[]{:S(2)}, u32[]{:S(2)}) async-start(bf16[4,32,4096]{2,1,0:T(8,128)(2,1)} %bitcast), calls=%async_computation | async-start | bytes 2097152 | tf_op jit(solution)/shard_map/all_to_all | solution.py:29
  30.5 172.3 %all-to-all-start.1 = ((bf16[64,8,4096]{2,1,0:T(8,128)(2,1)}), bf16[64,8,4096]{2,1,0:T(8,128)(2,1)}, u32[]{:S(2)}, u32[]{:S(2)}) async-start(bf16[64,8,4096]{2,1,0:T(8,128)(2,1)} %fusion.11), calls=%async_computation.1 | async-start | bytes 8388608 | tf_op jit(solution)/shard_map/all_to_all | solution.py:46
  43.3 113.3 %collective-permute-start = (bf16[1,2,192,4096]{3,2,1,0:T(8,128)(2,1)}, bf16[1,2,192,4096]{3,2,1,0:T(8,128)(2,1)S(1)}, u32[]{:S(2)}, u32[]{:S(2)}) collective-permute-start(bf16[1,2,192,4096]{3,2,1,0:T(8,128)(2,1)} %param.14), channel_id=1, source_target_pairs={{0,2},{1,3},{2,0},{3,1},{4,6},{5,7},{6,4},{7,5},{8,10},{9,11},{10,... | collective-permute-start | bytes 9437192 | tf_op jit(solution)/shard_map/ppermute | solution.py:13
  43.4 151.1 %collective-permute-start.1 = (bf16[1,2,192,4096]{3,2,1,0:T(8,128)(2,1)}, bf16[1,2,192,4096]{3,2,1,0:T(8,128)(2,1)S(1)}, u32[]{:S(2)}, u32[]{:S(2)}) collective-permute-start(bf16[1,2,192,4096]{3,2,1,0:T(8,128)(2,1)} %param.14), channel_id=1, source_target_pairs={{0,1},{1,0},{2,3},{3,2},{4,5},{5,4},{6,7},{7,6},{8,9},{9,8},{10,11... | collective-permute-start | bytes 9437192 | tf_op jit(solution)/shard_map/ppermute | solution.py:14
  156.6 38.0 %collective-permute-start.2 = (bf16[1,2,192,4096]{3,2,1,0:T(8,128)(2,1)S(1)}, bf16[1,2,192,4096]{3,2,1,0:T(8,128)(2,1)S(1)}, u32[]{:S(2)}, u32[]{:S(2)}) collective-permute-start(bf16[1,2,192,4096]{3,2,1,0:T(8,128)(2,1)S(1)} %collective-permute-done), channel_id=1, source_target_pairs={{0,1},{1,0},{2,3},{3,2},{4,5},{5,4},{6,7},{7,6},{8,9},{9,8},{10,11... | collective-permute-start | bytes 9437192 | tf_op jit(solution)/shard_map/ppermute | solution.py:14
  157.4 36.3 %collective-permute-start.3 = (bf16[1,192,4096]{2,1,0:T(8,128)(2,1)}, bf16[1,192,4096]{2,1,0:T(8,128)(2,1)}, u32[]{:S(2)}, u32[]{:S(2)}) collective-permute-start(bf16[1,192,4096]{2,1,0:T(8,128)(2,1)} %param.15), channel_id=1, source_target_pairs={{0,2},{1,3},{2,0},{3,1},{4,6},{5,7},{6,4},{7,5},{8,10},{9,11},{10,... | collective-permute-start | bytes 4718600 | tf_op jit(solution)/shard_map/ppermute | solution.py:13
  158.7 55.8 %collective-permute-start.4 = (bf16[1,192,4096]{2,1,0:T(8,128)(2,1)}, bf16[1,192,4096]{2,1,0:T(8,128)(2,1)}, u32[]{:S(2)}, u32[]{:S(2)}) collective-permute-start(bf16[1,192,4096]{2,1,0:T(8,128)(2,1)} %param.15), channel_id=1, source_target_pairs={{0,1},{1,0},{2,3},{3,2},{4,5},{5,4},{6,7},{7,6},{8,9},{9,8},{10,11... | collective-permute-start | bytes 4718600 | tf_op jit(solution)/shard_map/ppermute | solution.py:14
  193.7 20.8 %collective-permute-start.5 = (bf16[1,192,4096]{2,1,0:T(8,128)(2,1)}, bf16[1,192,4096]{2,1,0:T(8,128)(2,1)}, u32[]{:S(2)}, u32[]{:S(2)}) collective-permute-start(bf16[1,192,4096]{2,1,0:T(8,128)(2,1)} %collective-permute-done.3), channel_id=1, source_target_pairs={{0,1},{1,0},{2,3},{3,2},{4,5},{5,4},{6,7},{7,6},{8,9},{9,8},{10,11... | collective-permute-start | bytes 4718600 | tf_op jit(solution)/shard_map/ppermute | solution.py:14
  213.4 1.4 copy-start.6
  221.5 12.8 %copy-start.5 = (f32[32,8]{0,1:T(8,128)S(1)}, f32[32,8]{0,1:T(8,128)}, u32[]{:S(2)}) copy-start(f32[32,8]{0,1:T(8,128)} %param.13) | copy-start | bytes 3076
  221.5 107.0 %all-to-all-start.2 = ((bf16[64,8,4096]{2,1,0:T(8,128)(2,1)}), bf16[64,8,4096]{2,1,0:T(8,128)(2,1)}, u32[]{:S(2)}, u32[]{:S(2)}) async-start(bf16[64,8,4096]{2,1,0:T(8,128)(2,1)} %fusion.12), calls=%async_computation.2 | async-start | bytes 8388608 | tf_op jit(solution)/shard_map/all_to_all | solution.py:60
  233.9 98.4 %copy-start.1 = (bf16[128,1024]{1,0:T(8,128)(2,1)S(1)}, bf16[128,1024]{1,0:T(8,128)(2,1)}, u32[]{:S(2)}) copy-start(bf16[128,1024]{1,0:T(8,128)(2,1)} %param.8) | copy-start | bytes 786436

commit v5 on v3

--- a/solution.py
+++ b/solution.py
@@ -11,7 +11,8 @@
     near_pairs = [(j, j ^ 1) for j in range(tp_size)]
     own = (w_gate_up, w_down)
     far = lax.ppermute(own, "tp", far_pairs)
-    near_own, near_far = lax.ppermute((own, far), "tp", near_pairs)
+    near_own = lax.ppermute(own, "tp", near_pairs)
+    near_far = lax.ppermute(far, "tp", near_pairs)
     return [own, far, near_own, near_far]
 
 
@@ -25,11 +26,11 @@
     pieces = gather_weights(w_gate_up, w_down)
     attn_part = jnp.dot(context, wo_proj, preferred_element_type=jnp.float32)
     attn = lax.psum_scatter(
-        attn_part,
+        attn_part.astype(jnp.bfloat16),
         "tp",
         scatter_dimension=0,
         tiled=True,
-    )
+    ).astype(jnp.float32)
     hidden = residual.astype(jnp.float32) + attn
     inverse_rms = lax.rsqrt(jnp.mean(hidden * hidden, axis=1, keepdims=True) + 1e-06)
     normed = (hidden * inverse_rms * norm_gain.astype(jnp.float32)).astype(jnp.bfloat16)

time: 385 us -> 377 us (0.979)
  waiting for transfers between devices: 274 us -> 266 us
    reduce_scatter x1, waiting for transfers between devices: 33.4 us -> 25.7 us  [layer(): lax.psum_scatter(attn_part.astype(jnp.bfloat16), 'tp', scatter_dimension=...]
where the time goes in v5:
time: 377 us; the launch traced here: 375 us
  waiting for transfers between devices  266 us (71%)
  other arithmetic  32.3 us (9%)
  matrix products  30.1 us (8%)
  starting transfers between devices  29.8 us (8%)
  between operations  13.6 us (4%)
    ppermute x2, waiting for transfers between devices, gather_weights(): far = lax.ppermute(own, 'tp', far_pairs)  147 us
    all_to_all x1, waiting for transfers between devices, layer(): lax.all_to_all(expert_out.reshape(ep_size, exp_local * capacity, model_wi...  93.8 us
    concatenate x1, other arithmetic, layer(): jnp.concatenate([piece.reshape(-1, model_width) for piece, _ in pieces],...  28.7 us
    reduce_scatter x1, waiting for transfers between devices, layer(): lax.psum_scatter(attn_part.astype(jnp.bfloat16), 'tp', scatter_dimension=...  25.7 us
    all_to_all x1, starting transfers between devices, layer(): lax.all_to_all(send_rows, 'ep', split_axis=0, concat_axis=0, tiled=True)  12.8 us
    all_to_all x1, starting transfers between devices, layer(): lax.all_to_all(expert_out.reshape(ep_size, exp_local * capacity, model_wi...  12.8 us
    dot_general x1, matrix products, layer(): both = jnp.dot(rows, gate_up_full.T, preferred_element_type=jnp.float32)  10.6 us
  transfers between devices with their start and end apart: 9, of which 4 were waited for; matrix products, arithmetic and copies ran while one was open for 11% of the time, Pallas kernels for 0%

profile of v5, /device:TPU:1, one launch (start us, length us, event | category | flops | bytes accessed | tf_op | source)
XLA Modules:
  0.0 374.9 jit_solution(6125941264153023393)
XLA Ops:
  6.6 0.9 copy-done
  7.5 5.6 %convolution_convert_fusion.1 = bf16[128,4096]{1,0:T(8,128)(2,1)} fusion(bf16[128,1024]{1,0:T(8,128)(2,1)S(1)} %copy-done, bf16[1024,4096]{1,0:T(8,128)(2,1)} %param.9), kind=kOutput, calls=%fused_computation.13 | convolution fusion | flops 1074266112 | bytes 9699328 | tf_op jit(solution)/shard_map/dot_general | solution.py:27
  13.2 0.1 eq.160
  13.3 0.1 eq.164
  13.4 0.6 reduce-window.6
  14.0 0.2 slice_reduce_fusion
  14.3 0.1 fusion.30
  14.5 0.2 fusion.25
  14.7 25.7 %reduce-scatter.2.cloned.1.call-done = bf16[32,4096]{1,0:T(8,128)(2,1)} async-done(((bf16[128,4096]{1,0:T(8,128)(2,1)}), bf16[32,4096]{1,0:T(8,128)(2,1)}) %reduce-scatter.2.cloned.1.call-update) | async-done | bytes 262160 | tf_op jit(solution)/shard_map/reduce_scatter | solution.py:28
  40.5 1.1 multiply_reduce_fusion
  41.6 4.2 %fusion.11 = bf16[64,8,4096]{2,1,0:T(8,128)(2,1)} fusion(pred[512,32]{0,1:T(8,128)(4,1)S(1)} %fusion.25, bf16[32,4096]{1,0:T(8,128)(2,1)} %reduce-scatter.2.cloned.1.call-done, bf16[32,4096]{1,0:T(8,128)(2,1)S(1)} %copy-done.3, f32[4096]{0:T(1024)S(1)} %convert_element_type.53, f32[32]{0:T(128)S(1)} %add_rsqrt_fusion), kind=kOutput, calls=%fused_computation.11 | convolution fusion | flops 137101312 | bytes 4751488 | tf_op jit(solution)/shard_map/dot_general | solution.py:47
  45.8 12.8 %all-to-all-start = ((bf16[64,8,4096]{2,1,0:T(8,128)(2,1)}), bf16[64,8,4096]{2,1,0:T(8,128)(2,1)}, u32[]{:S(2)}, u32[]{:S(2)}) async-start(bf16[64,8,4096]{2,1,0:T(8,128)(2,1)} %fusion.11), calls=%async_computation.1 | async-start | bytes 8388608 | tf_op jit(solution)/shard_map/all_to_all | solution.py:49
  58.7 0.1 collective-permute-start
  58.8 0.6 collective-permute-start.1
  59.4 112.3 %collective-permute-done = bf16[1,2,192,4096]{3,2,1,0:T(8,128)(2,1)S(1)} collective-permute-done((bf16[1,2,192,4096]{3,2,1,0:T(8,128)(2,1)S(1)}, bf16[1,2,192,4096]{3,2,1,0:T(8,128)(2,1)S(1)}, u32[]{:S(2)}, u32[]{:S(2)}) %collective-permute-start) | collective-permute-done | bytes 3145760 | tf_op jit(solution)/shard_map/ppermute | solution.py:13
  171.6 0.9 collective-permute-start.2
  172.5 1.5 collective-permute-start.3
  174.0 0.3 collective-permute-start.4
  174.3 34.5 %collective-permute-done.3 = bf16[1,192,4096]{2,1,0:T(8,128)(2,1)} collective-permute-done((bf16[1,192,4096]{2,1,0:T(8,128)(2,1)}, bf16[1,192,4096]{2,1,0:T(8,128)(2,1)}, u32[]{:S(2)}, u32[]{:S(2)}) %collective-permute-start.3) | collective-permute-done | bytes 1572896 | tf_op jit(solution)/shard_map/ppermute | solution.py:13
  208.8 0.8 collective-permute-start.5
  209.7 28.7 %pad_maximum_fusion = bf16[1536,4096]{1,0:T(8,128)(2,1)} fusion(bf16[384,4096]{1,0:T(8,128)(2,1)S(1)} %bitcast.84, bf16[384,4096]{1,0:T(8,128)(2,1)S(1)} %bitcast.83, bf16[384,4096]{1,0:T(8,128)(2,1)S(1)} %bitcast.82, bf16[384,4096]{1,0:T(8,128)(2,1)S(1)} %bitcast.81), kind=kLoop, calls=%fused_computation | loop fusion | flops 50331648 | bytes 25165824 | tf_op jit(solution)/shard_map/concatenate | solution.py:53
  238.3 10.6 %fusion.15 = f32[512,4,2,192]{0,3,2,1:T(8,128)S(1)} fusion(bf16[4,2,192,4096]{3,2,1,0:T(8,128)(2,1)} %bitcast.80, bf16[64,8,4096]{2,1,0:T(8,128)(2,1)} %all-to-all-done), kind=kOutput, calls=%fused_computation.14 | convolution fusion | flops 6442450944 | bytes 19922944 | tf_op jit(solution)/shard_map/dot_general | solution.py:57
  249.0 0.5 fusion.39
  249.5 0.5 fusion.19
  250.0 0.3 copy-done.9
  250.4 6.7 %fusion.12 = bf16[64,8,4096]{2,1,0:T(8,128)(2,1)} fusion(bf16[512,768]{0,1:T(8,128)(2,1)S(1)} %fusion.19, bf16[192,4096]{1,0:T(8,128)(2,1)} %bitcast.23, bf16[192,4096]{1,0:T(8,128)(2,1)} %bitcast.22, bf16[192,4096]{1,0:T(8,128)(2,1)} %bitcast.21, bf16[192,4096]{1,0:T(8,128)(2,1)S(1)} %bitcast.85), kind=kOutput, calls=%fused_computation.12 | convolution fusion | flops 3248488448 | bytes 11272192 | tf_op jit(solution)/shard_map/dot_general | solution.py:60
  257.0 12.8 %all-to-all-start.1 = ((bf16[64,8,4096]{2,1,0:T(8,128)(2,1)}), bf16[64,8,4096]{2,1,0:T(8,128)(2,1)}, u32[]{:S(2)}, u32[]{:S(2)}) async-start(bf16[64,8,4096]{2,1,0:T(8,128)(2,1)} %fusion.12), calls=%async_computation.2 | async-start | bytes 8388608 | tf_op jit(solution)/shard_map/all_to_all | solution.py:63
  269.8 0.3 slice_reduce_fusion.8
  270.2 0.1 subtract_convert_fusion
  270.3 93.8 %all-to-all-done.1 = bf16[64,8,4096]{2,1,0:T(8,128)(2,1)} async-done(((bf16[64,8,4096]{2,1,0:T(8,128)(2,1)}), bf16[64,8,4096]{2,1,0:T(8,128)(2,1)}, u32[]{:S(2)}, u32[]{:S(2)}) %all-to-all-start.1) | async-done | bytes 4194336 | tf_op jit(solution)/shard_map/all_to_all | solution.py:63
  364.1 3.0 fusion.17
  367.2 0.8 fusion.24
  (34 shorter events, 0.3 us)
Async XLA Ops:
  6.5 1.0 copy-start
  6.5 6.6 %copy-start.7 = (s32[32,8]{0,1:T(8,128)S(1)}, s32[32,8]{0,1:T(8,128)}, u32[]{:S(2)}) copy-start(s32[32,8]{0,1:T(8,128)} %param.12) | copy-start | bytes 3076
  6.5 7.9 %copy-start.6 = (bf16[4096]{0:T(1024)(128)(2,1)S(1)}, bf16[4096]{0:T(1024)(128)(2,1)}, u32[]{:S(2)}) copy-start(bf16[4096]{0:T(1024)(128)(2,1)} %param.11) | copy-start | bytes 24580
  6.5 33.9 %copy-start.3 = (bf16[32,4096]{1,0:T(8,128)(2,1)S(1)}, bf16[32,4096]{1,0:T(8,128)(2,1)}, u32[]{:S(2)}) copy-start(bf16[32,4096]{1,0:T(8,128)(2,1)} %param.10) | copy-start | bytes 786436
  6.5 33.9 %reduce-scatter.2.cloned.1.call-start = ((), (), s32[]{:S(2)}) async-start(), calls=%async_computation.3 | async-start | bytes 1310720 | tf_op jit(solution)/shard_map/reduce_scatter | solution.py:28
  45.8 12.8 %copy-start.2 = (bf16[1,2,192,4096]{3,2,1,0:T(8,128)(2,1)S(1)}, bf16[1,2,192,4096]{3,2,1,0:T(8,128)(2,1)}, u32[]{:S(2)}) copy-start(bf16[1,2,192,4096]{3,2,1,0:T(8,128)(2,1)} %param.14) | copy-start | bytes 9437188
  45.8 192.5 %all-to-all-start = ((bf16[64,8,4096]{2,1,0:T(8,128)(2,1)}), bf16[64,8,4096]{2,1,0:T(8,128)(2,1)}, u32[]{:S(2)}, u32[]{:S(2)}) async-start(bf16[64,8,4096]{2,1,0:T(8,128)(2,1)} %fusion.11), calls=%async_computation.1 | async-start | bytes 8388608 | tf_op jit(solution)/shard_map/all_to_all | solution.py:49
  58.7 113.0 %collective-permute-start = (bf16[1,2,192,4096]{3,2,1,0:T(8,128)(2,1)S(1)}, bf16[1,2,192,4096]{3,2,1,0:T(8,128)(2,1)S(1)}, u32[]{:S(2)}, u32[]{:S(2)}) collective-permute-start(bf16[1,2,192,4096]{3,2,1,0:T(8,128)(2,1)S(1)} %copy-done.2), channel_id=1, source_target_pairs={{0,2},{1,3},{2,0},{3,1},{4,6},{5,7},{6,4},{7,5},{8,10},{9,11},{10,... | collective-permute-start | bytes 9437192 | tf_op jit(solution)/shard_map/ppermute | solution.py:13
  58.8 150.9 %collective-permute-start.1 = (bf16[1,2,192,4096]{3,2,1,0:T(8,128)(2,1)S(1)}, bf16[1,2,192,4096]{3,2,1,0:T(8,128)(2,1)S(1)}, u32[]{:S(2)}, u32[]{:S(2)}) collective-permute-start(bf16[1,2,192,4096]{3,2,1,0:T(8,128)(2,1)S(1)} %copy-done.2), channel_id=1, source_target_pairs={{0,1},{1,0},{2,3},{3,2},{4,5},{5,4},{6,7},{7,6},{8,9},{9,8},{10,11... | collective-permute-start | bytes 9437192 | tf_op jit(solution)/shard_map/ppermute | solution.py:14
  171.6 38.0 %collective-permute-start.2 = (bf16[1,2,192,4096]{3,2,1,0:T(8,128)(2,1)S(1)}, bf16[1,2,192,4096]{3,2,1,0:T(8,128)(2,1)S(1)}, u32[]{:S(2)}, u32[]{:S(2)}) collective-permute-start(bf16[1,2,192,4096]{3,2,1,0:T(8,128)(2,1)S(1)} %collective-permute-done), channel_id=1, source_target_pairs={{0,1},{1,0},{2,3},{3,2},{4,5},{5,4},{6,7},{7,6},{8,9},{9,8},{10,11... | collective-permute-start | bytes 9437192 | tf_op jit(solution)/shard_map/ppermute | solution.py:15
  172.5 36.3 %collective-permute-start.3 = (bf16[1,192,4096]{2,1,0:T(8,128)(2,1)}, bf16[1,192,4096]{2,1,0:T(8,128)(2,1)}, u32[]{:S(2)}, u32[]{:S(2)}) collective-permute-start(bf16[1,192,4096]{2,1,0:T(8,128)(2,1)} %param.15), channel_id=1, source_target_pairs={{0,2},{1,3},{2,0},{3,1},{4,6},{5,7},{6,4},{7,5},{8,10},{9,11},{10,... | collective-permute-start | bytes 4718600 | tf_op jit(solution)/shard_map/ppermute | solution.py:13
  174.0 76.0 %collective-permute-start.4 = (bf16[1,192,4096]{2,1,0:T(8,128)(2,1)}, bf16[1,192,4096]{2,1,0:T(8,128)(2,1)}, u32[]{:S(2)}, u32[]{:S(2)}) collective-permute-start(bf16[1,192,4096]{2,1,0:T(8,128)(2,1)} %param.15), channel_id=1, source_target_pairs={{0,1},{1,0},{2,3},{3,2},{4,5},{5,4},{6,7},{7,6},{8,9},{9,8},{10,11... | collective-permute-start | bytes 4718600 | tf_op jit(solution)/shard_map/ppermute | solution.py:14
  208.8 41.2 %collective-permute-start.5 = (bf16[1,192,4096]{2,1,0:T(8,128)(2,1)}, bf16[1,192,4096]{2,1,0:T(8,128)(2,1)}, u32[]{:S(2)}, u32[]{:S(2)}) collective-permute-start(bf16[1,192,4096]{2,1,0:T(8,128)(2,1)} %collective-permute-done.3), channel_id=1, source_target_pairs={{0,1},{1,0},{2,3},{3,2},{4,5},{5,4},{6,7},{7,6},{8,9},{9,8},{10,11... | collective-permute-start | bytes 4718600 | tf_op jit(solution)/shard_map/ppermute | solution.py:15
  248.9 1.4 copy-start.9
  257.0 13.1 %copy-start.8 = (f32[32,8]{0,1:T(8,128)S(1)}, f32[32,8]{0,1:T(8,128)}, u32[]{:S(2)}) copy-start(f32[32,8]{0,1:T(8,128)} %param.13) | copy-start | bytes 3076
  257.0 107.1 %all-to-all-start.1 = ((bf16[64,8,4096]{2,1,0:T(8,128)(2,1)}), bf16[64,8,4096]{2,1,0:T(8,128)(2,1)}, u32[]{:S(2)}, u32[]{:S(2)}) async-start(bf16[64,8,4096]{2,1,0:T(8,128)(2,1)} %fusion.12), calls=%async_computation.2 | async-start | bytes 8388608 | tf_op jit(solution)/shard_map/all_to_all | solution.py:63
  269.8 97.4 %copy-start.4 = (bf16[32,4096]{1,0:T(8,128)(2,1)S(1)}, bf16[32,4096]{1,0:T(8,128)(2,1)}, u32[]{:S(2)}) copy-start(bf16[32,4096]{1,0:T(8,128)(2,1)} %param.10) | copy-start | bytes 786436
  269.8 97.4 %copy-start.5 = (bf16[32,4096]{1,0:T(8,128)(2,1)S(1)}, bf16[32,4096]{1,0:T(8,128)(2,1)}, u32[]{:S(2)}) copy-start(bf16[32,4096]{1,0:T(8,128)(2,1)} %reduce-scatter.2.cloned.1.call-done) | copy-start | bytes 786436
  269.8 98.2 %copy-start.1 = (bf16[128,1024]{1,0:T(8,128)(2,1)S(1)}, bf16[128,1024]{1,0:T(8,128)(2,1)}, u32[]{:S(2)}) copy-start(bf16[128,1024]{1,0:T(8,128)(2,1)} %param.8) | copy-start | bytes 786436
Sparse Core Ops, SparseCore 0:
  13.3 27.1 reduce-scatter.1

commit v6 on v5

--- a/solution.py
+++ b/solution.py
@@ -50,15 +50,16 @@
     received = received.reshape(ep_size, exp_local, capacity, model_width)
     slots = ep_size * exp_local * capacity
     rows = received.reshape(slots, model_width)
-    gate_up_full = jnp.concatenate(
-        [piece.reshape(-1, model_width) for piece, _ in pieces], axis=0
-    )
     down_full = jnp.concatenate([piece.reshape(-1, model_width) for _, piece in pieces], axis=0)
-    both = jnp.dot(rows, gate_up_full.T, preferred_element_type=jnp.float32)
-    both = both.reshape(slots, len(pieces), 2, -1)
-    activated = (jax.nn.silu(both[:, :, 0]) * both[:, :, 1]).astype(jnp.bfloat16)
+    activated = []
+    for gate_up_piece, _ in pieces:
+        both = jnp.dot(
+            rows, gate_up_piece.reshape(-1, model_width).T, preferred_element_type=jnp.float32
+        ).reshape(slots, 2, -1)
+        activated.append((jax.nn.silu(both[:, 0]) * both[:, 1]).astype(jnp.bfloat16))
+    activated = jnp.concatenate(activated, axis=1)
     expert_out = jnp.dot(
-        activated.reshape(slots, -1), down_full, preferred_element_type=jnp.float32
+        activated, down_full, preferred_element_type=jnp.float32
     ).astype(jnp.bfloat16)
     returned = lax.all_to_all(
         expert_out.reshape(ep_size, exp_local * capacity, model_width),

time: 377 us -> 357 us (0.947)
  other arithmetic: 32.3 us -> 3.61 us
  matrix products: 30.1 us -> 37.9 us
    concatenate x1 -> x0, other arithmetic: 28.7 us -> none  [layer(): jnp.concatenate([piece.reshape(-1, model_width) for piece, _ in pieces],...]
    dot_general x2 -> x5, matrix products: 17.3 us -> 25 us  [the longest x4 18.4 us: layer(): jnp.dot(rows, gate_up_piece.reshape(-1, model_width).T, preferred_element...]
  transfers between devices with their start and end apart: 9 -> 9, of which waited for: 4 -> 4; matrix products, arithmetic and copies ran while one was open for 11% -> 6% of each run, Pallas kernels for 0% -> 0%
where the time goes in v6:
time: 357 us; the launch traced here: 355 us
  waiting for transfers between devices  267 us (75%)
  matrix products  37.9 us (11%)
  starting transfers between devices  29.2 us (8%)
  between operations  13.6 us (4%)
  other arithmetic  3.61 us (1%)
    ppermute x2, waiting for transfers between devices, gather_weights(): far = lax.ppermute(own, 'tp', far_pairs)  147 us
    all_to_all x1, waiting for transfers between devices, layer(): lax.all_to_all(expert_out.reshape(ep_size, exp_local * capacity, model_wi...  94 us
    reduce_scatter x1, waiting for transfers between devices, layer(): lax.psum_scatter(attn_part.astype(jnp.bfloat16), 'tp', scatter_dimension=...  25.7 us
    dot_general x4, matrix products, layer(): jnp.dot(rows, gate_up_piece.reshape(-1, model_width).T, preferred_element...  18.4 us
    all_to_all x1, starting transfers between devices, layer(): lax.all_to_all(send_rows, 'ep', split_axis=0, concat_axis=0, tiled=True)  12.7 us
    all_to_all x1, starting transfers between devices, layer(): lax.all_to_all(expert_out.reshape(ep_size, exp_local * capacity, model_wi...  12.7 us
  transfers between devices with their start and end apart: 9, of which 4 were waited for; matrix products, arithmetic and copies ran while one was open for 6% of the time, Pallas kernels for 0%

profile of v6, /device:TPU:1, one launch (start us, length us, event | category | flops | bytes accessed | tf_op | source)
XLA Modules:
  0.0 354.7 jit_solution(2319368951091567111)
XLA Ops:
  6.6 0.9 copy-done
  7.5 5.6 %convolution_convert_fusion.1 = bf16[128,4096]{1,0:T(8,128)(2,1)} fusion(bf16[128,1024]{1,0:T(8,128)(2,1)S(1)} %copy-done, bf16[1024,4096]{1,0:T(8,128)(2,1)} %param.9), kind=kOutput, calls=%fused_computation.12 | convolution fusion | flops 1074266112 | bytes 9699328 | tf_op jit(solution)/shard_map/dot_general | solution.py:27
  13.4 0.6 reduce-window.6
  14.0 0.2 slice_reduce_fusion
  14.5 0.2 fusion.38
  14.7 25.7 %reduce-scatter.2.cloned.1.call-done = bf16[32,4096]{1,0:T(8,128)(2,1)} async-done(((bf16[128,4096]{1,0:T(8,128)(2,1)}), bf16[32,4096]{1,0:T(8,128)(2,1)}) %reduce-scatter.2.cloned.1.call-update) | async-done | bytes 262160 | tf_op jit(solution)/shard_map/reduce_scatter | solution.py:28
  40.5 1.1 multiply_reduce_fusion
  41.6 4.2 %fusion.11 = bf16[64,8,4096]{2,1,0:T(8,128)(2,1)} fusion(pred[512,32]{0,1:T(8,128)(4,1)S(1)} %fusion.38, bf16[32,4096]{1,0:T(8,128)(2,1)} %reduce-scatter.2.cloned.1.call-done, bf16[32,4096]{1,0:T(8,128)(2,1)S(1)} %copy-done.1, f32[4096]{0:T(1024)S(1)} %convert_element_type.61, f32[32]{0:T(128)S(1)} %add_rsqrt_fusion), kind=kOutput, calls=%fused_computation.10 | convolution fusion | flops 137101312 | bytes 4751488 | tf_op jit(solution)/shard_map/dot_general | solution.py:47
  45.9 12.7 %all-to-all-start = ((bf16[64,8,4096]{2,1,0:T(8,128)(2,1)}), bf16[64,8,4096]{2,1,0:T(8,128)(2,1)}, u32[]{:S(2)}, u32[]{:S(2)}) async-start(bf16[64,8,4096]{2,1,0:T(8,128)(2,1)} %fusion.11), calls=%async_computation.1 | async-start | bytes 8388608 | tf_op jit(solution)/shard_map/all_to_all | solution.py:49
  58.7 112.9 %collective-permute-done = bf16[1,2,192,4096]{3,2,1,0:T(8,128)(2,1)S(1)} collective-permute-done((bf16[1,2,192,4096]{3,2,1,0:T(8,128)(2,1)}, bf16[1,2,192,4096]{3,2,1,0:T(8,128)(2,1)S(1)}, u32[]{:S(2)}, u32[]{:S(2)}) %collective-permute-start) | collective-permute-done | bytes 3145760 | tf_op jit(solution)/shard_map/ppermute | solution.py:13
  171.6 1.8 copy-done.7
  173.3 0.9 collective-permute-start.2
  174.3 1.4 collective-permute-start.3
  175.7 0.3 collective-permute-start.1
  175.9 0.2 collective-permute-start.4
  176.2 34.2 %collective-permute-done.3 = bf16[1,192,4096]{2,1,0:T(8,128)(2,1)} collective-permute-done((bf16[1,192,4096]{2,1,0:T(8,128)(2,1)S(1)}, bf16[1,192,4096]{2,1,0:T(8,128)(2,1)}, u32[]{:S(2)}, u32[]{:S(2)}) %collective-permute-start.3) | collective-permute-done | bytes 1572896 | tf_op jit(solution)/shard_map/ppermute | solution.py:13
  210.3 0.9 collective-permute-start.5
  211.2 5.1 %fusion.17 = f32[512,2,192]{0,2,1:T(8,128)S(1)} fusion(bf16[64,8,4096]{2,1,0:T(8,128)(2,1)} %all-to-all-done, bf16[1,2,192,4096]{3,2,1,0:T(8,128)(2,1)} %collective-permute-done.2), kind=kOutput, calls=%fused_computation.15 | convolution fusion | flops 1610612736 | bytes 8126464 | tf_op jit(solution)/shard_map/dot_general | solution.py:56
  216.3 0.1 fusion.40
  216.5 4.1 %fusion.21 = f32[512,2,192]{0,2,1:T(8,128)S(1)} fusion(bf16[64,8,4096]{2,1,0:T(8,128)(2,1)} %all-to-all-done, bf16[1,2,192,4096]{3,2,1,0:T(8,128)(2,1)S(1)} %copy-done.8), kind=kOutput, calls=%fused_computation.19 | convolution fusion | flops 1610612736 | bytes 8126464 | tf_op jit(solution)/shard_map/dot_general | solution.py:56
  220.5 0.1 fusion.44
  220.7 5.1 %fusion.19 = f32[512,2,192]{0,2,1:T(8,128)S(1)} fusion(bf16[64,8,4096]{2,1,0:T(8,128)(2,1)} %all-to-all-done, bf16[1,2,192,4096]{3,2,1,0:T(8,128)(2,1)} %collective-permute-done.1), kind=kOutput, calls=%fused_computation.17 | convolution fusion | flops 1610612736 | bytes 8126464 | tf_op jit(solution)/shard_map/dot_general | solution.py:56
  225.8 0.1 fusion.42
  225.9 4.1 %fusion.23 = f32[512,2,192]{0,2,1:T(8,128)S(1)} fusion(bf16[64,8,4096]{2,1,0:T(8,128)(2,1)} %all-to-all-done, bf16[1,2,192,4096]{3,2,1,0:T(8,128)(2,1)S(1)} %copy-done.6), kind=kOutput, calls=%fused_computation.21 | convolution fusion | flops 1610612736 | bytes 8126464 | tf_op jit(solution)/shard_map/dot_general | solution.py:56
  230.0 0.1 fusion.46
  230.2 6.7 %fusion.12 = bf16[64,8,4096]{2,1,0:T(8,128)(2,1)} fusion(bf16[192,4096]{1,0:T(8,128)(2,1)} %bitcast.28, bf16[192,4096]{1,0:T(8,128)(2,1)} %bitcast.27, bf16[192,4096]{1,0:T(8,128)(2,1)} %bitcast.26, bf16[192,4096]{1,0:T(8,128)(2,1)S(1)} %bitcast.112, bf16[512,192]{0,1:T(8,128)(2,1)S(1)} %fusion.40, bf16[512,192]{0,1:T(8,128)(2,1)S(1)} %fusion.42, ...), kind=kOutput, calls=%fused_computation.11 | convolution fusion | flops 3251634176 | bytes 11272192 | tf_op jit(solution)/shard_map/dot_general | solution.py:61
  236.8 12.7 %all-to-all-start.1 = ((bf16[64,8,4096]{2,1,0:T(8,128)(2,1)}), bf16[64,8,4096]{2,1,0:T(8,128)(2,1)}, u32[]{:S(2)}, u32[]{:S(2)}) async-start(bf16[64,8,4096]{2,1,0:T(8,128)(2,1)} %fusion.12), calls=%async_computation.2 | async-start | bytes 8388608 | tf_op jit(solution)/shard_map/all_to_all | solution.py:64
  249.5 0.3 slice_reduce_fusion.8
  249.9 0.1 subtract_convert_fusion
  250.0 94.0 %all-to-all-done.1 = bf16[64,8,4096]{2,1,0:T(8,128)(2,1)} async-done(((bf16[64,8,4096]{2,1,0:T(8,128)(2,1)}), bf16[64,8,4096]{2,1,0:T(8,128)(2,1)}, u32[]{:S(2)}, u32[]{:S(2)}) %all-to-all-start.1) | async-done | bytes 4194336 | tf_op jit(solution)/shard_map/all_to_all | solution.py:64
  344.0 3.0 fusion.15
  347.0 0.8 fusion.37
  (38 shorter events, 0.7 us)
Async XLA Ops:
  6.5 1.0 copy-start
  6.5 6.6 %copy-start.4 = (s32[32,8]{0,1:T(8,128)S(1)}, s32[32,8]{0,1:T(8,128)}, u32[]{:S(2)}) copy-start(s32[32,8]{0,1:T(8,128)} %param.12) | copy-start | bytes 3076
  6.5 7.9 %copy-start.3 = (bf16[4096]{0:T(1024)(128)(2,1)S(1)}, bf16[4096]{0:T(1024)(128)(2,1)}, u32[]{:S(2)}) copy-start(bf16[4096]{0:T(1024)(128)(2,1)} %param.11) | copy-start | bytes 24580
  6.5 33.9 %copy-start.1 = (bf16[32,4096]{1,0:T(8,128)(2,1)S(1)}, bf16[32,4096]{1,0:T(8,128)(2,1)}, u32[]{:S(2)}) copy-start(bf16[32,4096]{1,0:T(8,128)(2,1)} %param.10) | copy-start | bytes 786436
  6.5 33.9 %reduce-scatter.2.cloned.1.call-start = ((), (), s32[]{:S(2)}) async-start(), calls=%async_computation.3 | async-start | bytes 1310720 | tf_op jit(solution)/shard_map/reduce_scatter | solution.py:28
  45.9 128.4 %copy-start.9 = (bf16[1,192,4096]{2,1,0:T(8,128)(2,1)S(1)}, bf16[1,192,4096]{2,1,0:T(8,128)(2,1)}, u32[]{:S(2)}) copy-start(bf16[1,192,4096]{2,1,0:T(8,128)(2,1)} %param.15) | copy-start | bytes 4718596
  45.9 165.3 %all-to-all-start = ((bf16[64,8,4096]{2,1,0:T(8,128)(2,1)}), bf16[64,8,4096]{2,1,0:T(8,128)(2,1)}, u32[]{:S(2)}, u32[]{:S(2)}) async-start(bf16[64,8,4096]{2,1,0:T(8,128)(2,1)} %fusion.11), calls=%async_computation.1 | async-start | bytes 8388608 | tf_op jit(solution)/shard_map/all_to_all | solution.py:49
  58.6 113.0 %collective-permute-start = (bf16[1,2,192,4096]{3,2,1,0:T(8,128)(2,1)}, bf16[1,2,192,4096]{3,2,1,0:T(8,128)(2,1)S(1)}, u32[]{:S(2)}, u32[]{:S(2)}) collective-permute-start(bf16[1,2,192,4096]{3,2,1,0:T(8,128)(2,1)} %param.14), channel_id=1, source_target_pairs={{0,2},{1,3},{2,0},{3,1},{4,6},{5,7},{6,4},{7,5},{8,10},{9,11},{10,... | collective-permute-start | bytes 9437192 | tf_op jit(solution)/shard_map/ppermute | solution.py:13
  171.6 1.8 copy-start.7
  173.3 37.9 %collective-permute-start.2 = (bf16[1,2,192,4096]{3,2,1,0:T(8,128)(2,1)S(1)}, bf16[1,2,192,4096]{3,2,1,0:T(8,128)(2,1)}, u32[]{:S(2)}, u32[]{:S(2)}) collective-permute-start(bf16[1,2,192,4096]{3,2,1,0:T(8,128)(2,1)S(1)} %collective-permute-done), channel_id=1, source_target_pairs={{0,1},{1,0},{2,3},{3,2},{4,5},{5,4},{6,7},{7,6},{8,9},{9,8},{10,11... | collective-permute-start | bytes 9437192 | tf_op jit(solution)/shard_map/ppermute | solution.py:15
  174.3 36.1 %collective-permute-start.3 = (bf16[1,192,4096]{2,1,0:T(8,128)(2,1)S(1)}, bf16[1,192,4096]{2,1,0:T(8,128)(2,1)}, u32[]{:S(2)}, u32[]{:S(2)}) collective-permute-start(bf16[1,192,4096]{2,1,0:T(8,128)(2,1)S(1)} %copy-done.9), channel_id=1, source_target_pairs={{0,2},{1,3},{2,0},{3,1},{4,6},{5,7},{6,4},{7,5},{8,10},{9,11},{10,... | collective-permute-start | bytes 4718600 | tf_op jit(solution)/shard_map/ppermute | solution.py:13
  175.7 45.0 %collective-permute-start.1 = (bf16[1,2,192,4096]{3,2,1,0:T(8,128)(2,1)}, bf16[1,2,192,4096]{3,2,1,0:T(8,128)(2,1)}, u32[]{:S(2)}, u32[]{:S(2)}) collective-permute-start(bf16[1,2,192,4096]{3,2,1,0:T(8,128)(2,1)} %param.14), channel_id=1, source_target_pairs={{0,1},{1,0},{2,3},{3,2},{4,5},{5,4},{6,7},{7,6},{8,9},{9,8},{10,11... | collective-permute-start | bytes 9437192 | tf_op jit(solution)/shard_map/ppermute | solution.py:14
  175.9 54.2 %collective-permute-start.4 = (bf16[1,192,4096]{2,1,0:T(8,128)(2,1)S(1)}, bf16[1,192,4096]{2,1,0:T(8,128)(2,1)}, u32[]{:S(2)}, u32[]{:S(2)}) collective-permute-start(bf16[1,192,4096]{2,1,0:T(8,128)(2,1)S(1)} %copy-done.9), channel_id=1, source_target_pairs={{0,1},{1,0},{2,3},{3,2},{4,5},{5,4},{6,7},{7,6},{8,9},{9,8},{10,11... | collective-permute-start | bytes 4718600 | tf_op jit(solution)/shard_map/ppermute | solution.py:14
  210.3 19.8 %collective-permute-start.5 = (bf16[1,192,4096]{2,1,0:T(8,128)(2,1)}, bf16[1,192,4096]{2,1,0:T(8,128)(2,1)}, u32[]{:S(2)}, u32[]{:S(2)}) collective-permute-start(bf16[1,192,4096]{2,1,0:T(8,128)(2,1)} %collective-permute-done.3), channel_id=1, source_target_pairs={{0,1},{1,0},{2,3},{3,2},{4,5},{5,4},{6,7},{7,6},{8,9},{9,8},{10,11... | collective-permute-start | bytes 4718600 | tf_op jit(solution)/shard_map/ppermute | solution.py:15
  211.2 5.3 %copy-start.8 = (bf16[1,2,192,4096]{3,2,1,0:T(8,128)(2,1)S(1)}, bf16[1,2,192,4096]{3,2,1,0:T(8,128)(2,1)}, u32[]{:S(2)}) copy-start(bf16[1,2,192,4096]{3,2,1,0:T(8,128)(2,1)} %copy-done.7) | copy-start | bytes 9437188
  220.7 5.3 %copy-start.6 = (bf16[1,2,192,4096]{3,2,1,0:T(8,128)(2,1)S(1)}, bf16[1,2,192,4096]{3,2,1,0:T(8,128)(2,1)}, u32[]{:S(2)}) copy-start(bf16[1,2,192,4096]{3,2,1,0:T(8,128)(2,1)} %param.14) | copy-start | bytes 9437188
  236.8 13.0 %copy-start.5 = (f32[32,8]{0,1:T(8,128)S(1)}, f32[32,8]{0,1:T(8,128)}, u32[]{:S(2)}) copy-start(f32[32,8]{0,1:T(8,128)} %param.13) | copy-start | bytes 3076
  236.8 107.2 %all-to-all-start.1 = ((bf16[64,8,4096]{2,1,0:T(8,128)(2,1)}), bf16[64,8,4096]{2,1,0:T(8,128)(2,1)}, u32[]{:S(2)}, u32[]{:S(2)}) async-start(bf16[64,8,4096]{2,1,0:T(8,128)(2,1)} %fusion.12), calls=%async_computation.2 | async-start | bytes 8388608 | tf_op jit(solution)/shard_map/all_to_all | solution.py:64
  249.5 97.5 %copy-start.2 = (bf16[32,4096]{1,0:T(8,128)(2,1)S(1)}, bf16[32,4096]{1,0:T(8,128)(2,1)}, u32[]{:S(2)}) copy-start(bf16[32,4096]{1,0:T(8,128)(2,1)} %reduce-scatter.2.cloned.1.call-done) | copy-start | bytes 786436
Sparse Core Ops, SparseCore 0:
  13.3 27.1 reduce-scatter.1

commit v7 on v6

--- a/solution.py
+++ b/solution.py
@@ -10,7 +10,9 @@
     far_pairs = [(j, j ^ half) for j in range(tp_size)]
     near_pairs = [(j, j ^ 1) for j in range(tp_size)]
     own = (w_gate_up, w_down)
-    far = lax.ppermute(own, "tp", far_pairs)
+    far_gu = lax.ppermute(w_gate_up, "tp", far_pairs)
+    far_dn = lax.ppermute(w_down, "tp", far_pairs)
+    far = (far_gu, far_dn)
     near_own = lax.ppermute(own, "tp", near_pairs)
     near_far = lax.ppermute(far, "tp", near_pairs)
     return [own, far, near_own, near_far]
@@ -25,12 +27,10 @@
     capacity = max(2, min(quarter_rows, 2 * quarter_rows * top_count // experts))
     pieces = gather_weights(w_gate_up, w_down)
     attn_part = jnp.dot(context, wo_proj, preferred_element_type=jnp.float32)
-    attn = lax.psum_scatter(
-        attn_part.astype(jnp.bfloat16),
-        "tp",
-        scatter_dimension=0,
-        tiled=True,
-    ).astype(jnp.float32)
+    tp_size = lax.axis_size("tp")
+    shares = attn_part.astype(jnp.bfloat16).reshape(tp_size, quarter_rows, model_width)
+    shares = lax.all_to_all(shares, "tp", split_axis=0, concat_axis=0, tiled=True)
+    attn = jnp.sum(shares.astype(jnp.float32), axis=0)
     hidden = residual.astype(jnp.float32) + attn
     inverse_rms = lax.rsqrt(jnp.mean(hidden * hidden, axis=1, keepdims=True) + 1e-06)
     normed = (hidden * inverse_rms * norm_gain.astype(jnp.float32)).astype(jnp.bfloat16)

time: 357 us -> 335 us (0.938)
  waiting for transfers between devices: 267 us -> 253 us
  between operations: 13.6 us -> 0.23 us
  starting transfers between devices: 29.2 us -> 35.8 us
    reduce_scatter x1 -> x0, waiting for transfers between devices: 25.7 us -> none  [layer(): lax.psum_scatter(attn_part.astype(jnp.bfloat16), 'tp', scatter_dimension=...]
    all_to_all x0 -> x1, waiting for transfers between devices: none -> 11.9 us  [layer(): lax.all_to_all(shares, 'tp', split_axis=0, concat_axis=0, tiled=True)]
    all_to_all x0 -> x1, starting transfers between devices: none -> 6.81 us  [layer(): lax.all_to_all(shares, 'tp', split_axis=0, concat_axis=0, tiled=True)]
where the time goes in v7:
time: 335 us; the launch traced here: 333 us
  waiting for transfers between devices  253 us (76%)
  matrix products  37 us (11%)
  starting transfers between devices  35.8 us (11%)
  local copies, waits for them, and re-layouts  3.57 us (1%)
    ppermute x1, waiting for transfers between devices, gather_weights(): far_gu = lax.ppermute(w_gate_up, 'tp', far_pairs)  113 us
    all_to_all x1, waiting for transfers between devices, layer(): lax.all_to_all(expert_out.reshape(ep_size, exp_local * capacity, model_wi...  94 us
    ppermute x1, waiting for transfers between devices, gather_weights(): far_dn = lax.ppermute(w_down, 'tp', far_pairs)  34.3 us
    dot_general x4, matrix products, layer(): jnp.dot(rows, gate_up_piece.reshape(-1, model_width).T, preferred_element...  18.4 us
    all_to_all x1, starting transfers between devices, layer(): lax.all_to_all(send_rows, 'ep', split_axis=0, concat_axis=0, tiled=True)  13 us
    all_to_all x1, starting transfers between devices, layer(): lax.all_to_all(expert_out.reshape(ep_size, exp_local * capacity, model_wi...  12.5 us
    all_to_all x1, waiting for transfers between devices, layer(): lax.all_to_all(shares, 'tp', split_axis=0, concat_axis=0, tiled=True)  11.9 us
    all_to_all x1, starting transfers between devices, layer(): lax.all_to_all(shares, 'tp', split_axis=0, concat_axis=0, tiled=True)  6.81 us
  transfers between devices with their start and end apart: 9, of which 4 were waited for; matrix products, arithmetic and copies ran while one was open for 6% of the time, Pallas kernels for 0%

profile of v7, /device:TPU:1, one launch (start us, length us, event | category | flops | bytes accessed | tf_op | source)
XLA Modules:
  0.0 332.7 jit_solution(17457578273672851102)
XLA Ops:
  0.0 0.9 copy-done
  1.0 5.6 %convolution_convert_fusion.1 = bf16[128,4096]{1,0:T(8,128)(2,1)} fusion(bf16[128,1024]{1,0:T(8,128)(2,1)S(1)} %copy-done, bf16[1024,4096]{1,0:T(8,128)(2,1)} %param.9), kind=kOutput, calls=%fused_computation.12 | convolution fusion | flops 1074266112 | bytes 9699328 | tf_op jit(solution)/shard_map/dot_general | solution.py:29
  6.6 6.8 %all-to-all-start = ((bf16[4,32,4096]{2,1,0:T(8,128)(2,1)}), bf16[4,32,4096]{2,1,0:T(8,128)(2,1)S(1)}, u32[]{:S(2)}, u32[]{:S(2)}) async-start(bf16[4,32,4096]{2,1,0:T(8,128)(2,1)} %bitcast), calls=%async_computation | async-start | bytes 2097152 | tf_op jit(solution)/shard_map/all_to_all | solution.py:32
  13.7 0.6 reduce-window.6
  14.3 0.2 slice_reduce_fusion
  14.8 0.2 fusion.38
  15.0 11.9 %all-to-all-done = bf16[4,32,4096]{2,1,0:T(8,128)(2,1)S(1)} async-done(((bf16[4,32,4096]{2,1,0:T(8,128)(2,1)}), bf16[4,32,4096]{2,1,0:T(8,128)(2,1)S(1)}, u32[]{:S(2)}, u32[]{:S(2)}) %all-to-all-start) | async-done | bytes 1048608 | tf_op jit(solution)/shard_map/all_to_all | solution.py:32
  26.9 0.2 convert_reduce_fusion
  27.0 0.2 multiply_reduce_fusion
  27.2 3.3 fusion.11
  30.5 13.0 %all-to-all-start.1 = ((bf16[64,8,4096]{2,1,0:T(8,128)(2,1)}), bf16[64,8,4096]{2,1,0:T(8,128)(2,1)}, u32[]{:S(2)}, u32[]{:S(2)}) async-start(bf16[64,8,4096]{2,1,0:T(8,128)(2,1)} %fusion.11), calls=%async_computation.1 | async-start | bytes 8388608 | tf_op jit(solution)/shard_map/all_to_all | solution.py:49
  43.6 113.2 %collective-permute-done = bf16[1,2,192,4096]{3,2,1,0:T(8,128)(2,1)S(1)} collective-permute-done((bf16[1,2,192,4096]{3,2,1,0:T(8,128)(2,1)}, bf16[1,2,192,4096]{3,2,1,0:T(8,128)(2,1)S(1)}, u32[]{:S(2)}, u32[]{:S(2)}) %collective-permute-start) | collective-permute-done | bytes 3145760 | tf_op jit(solution)/shard_map/ppermute | solution.py:13
  156.8 1.8 copy-done.6
  158.5 0.8 collective-permute-start.2
  159.4 1.2 collective-permute-start.3
  160.6 0.3 collective-permute-start.1
  160.9 0.2 collective-permute-start.4
  161.1 34.3 %collective-permute-done.3 = bf16[1,192,4096]{2,1,0:T(8,128)(2,1)} collective-permute-done((bf16[1,192,4096]{2,1,0:T(8,128)(2,1)S(1)}, bf16[1,192,4096]{2,1,0:T(8,128)(2,1)}, u32[]{:S(2)}, u32[]{:S(2)}) %collective-permute-start.3) | collective-permute-done | bytes 1572896 | tf_op jit(solution)/shard_map/ppermute | solution.py:14
  195.4 0.9 collective-permute-start.5
  196.3 5.1 %fusion.17 = f32[512,2,192]{0,2,1:T(8,128)S(1)} fusion(bf16[64,8,4096]{2,1,0:T(8,128)(2,1)} %all-to-all-done.1, bf16[1,2,192,4096]{3,2,1,0:T(8,128)(2,1)} %collective-permute-done.2), kind=kOutput, calls=%fused_computation.15 | convolution fusion | flops 1610612736 | bytes 8126464 | tf_op jit(solution)/shard_map/dot_general | solution.py:56
  201.4 0.1 fusion.40
  201.5 4.1 %fusion.21 = f32[512,2,192]{0,2,1:T(8,128)S(1)} fusion(bf16[64,8,4096]{2,1,0:T(8,128)(2,1)} %all-to-all-done.1, bf16[1,2,192,4096]{3,2,1,0:T(8,128)(2,1)S(1)} %copy-done.7), kind=kOutput, calls=%fused_computation.19 | convolution fusion | flops 1610612736 | bytes 8126464 | tf_op jit(solution)/shard_map/dot_general | solution.py:56
  205.6 0.1 fusion.44
  205.8 5.1 %fusion.19 = f32[512,2,192]{0,2,1:T(8,128)S(1)} fusion(bf16[64,8,4096]{2,1,0:T(8,128)(2,1)} %all-to-all-done.1, bf16[1,2,192,4096]{3,2,1,0:T(8,128)(2,1)} %collective-permute-done.1), kind=kOutput, calls=%fused_computation.17 | convolution fusion | flops 1610612736 | bytes 8126464 | tf_op jit(solution)/shard_map/dot_general | solution.py:56
  211.0 4.1 %fusion.23 = f32[512,2,192]{0,2,1:T(8,128)S(1)} fusion(bf16[64,8,4096]{2,1,0:T(8,128)(2,1)} %all-to-all-done.1, bf16[1,2,192,4096]{3,2,1,0:T(8,128)(2,1)S(1)} %copy-done.5), kind=kOutput, calls=%fused_computation.21 | convolution fusion | flops 1610612736 | bytes 8126464 | tf_op jit(solution)/shard_map/dot_general | solution.py:56
  215.2 6.7 %fusion.12 = bf16[64,8,4096]{2,1,0:T(8,128)(2,1)} fusion(bf16[192,4096]{1,0:T(8,128)(2,1)} %bitcast.29, bf16[192,4096]{1,0:T(8,128)(2,1)} %bitcast.28, bf16[192,4096]{1,0:T(8,128)(2,1)} %bitcast.27, bf16[192,4096]{1,0:T(8,128)(2,1)S(1)} %bitcast.113, bf16[512,192]{0,1:T(8,128)(2,1)S(1)} %fusion.40, bf16[512,192]{0,1:T(8,128)(2,1)S(1)} %fusion.42, ...), kind=kOutput, calls=%fused_computation.11 | convolution fusion | flops 3251634176 | bytes 11272192 | tf_op jit(solution)/shard_map/dot_general | solution.py:61
  221.9 12.5 %all-to-all-start.2 = ((bf16[64,8,4096]{2,1,0:T(8,128)(2,1)}), bf16[64,8,4096]{2,1,0:T(8,128)(2,1)}, u32[]{:S(2)}, u32[]{:S(2)}) async-start(bf16[64,8,4096]{2,1,0:T(8,128)(2,1)} %fusion.12), calls=%async_computation.2 | async-start | bytes 8388608 | tf_op jit(solution)/shard_map/all_to_all | solution.py:64
  234.4 0.3 slice_reduce_fusion.8
  234.7 0.1 subtract_convert_fusion
  234.8 94.0 %all-to-all-done.2 = bf16[64,8,4096]{2,1,0:T(8,128)(2,1)} async-done(((bf16[64,8,4096]{2,1,0:T(8,128)(2,1)}), bf16[64,8,4096]{2,1,0:T(8,128)(2,1)}, u32[]{:S(2)}, u32[]{:S(2)}) %all-to-all-start.2) | async-done | bytes 4194336 | tf_op jit(solution)/shard_map/all_to_all | solution.py:64
  328.8 3.0 fusion.15
  331.9 0.8 fusion.37
  (36 shorter events, 0.9 us)
Async XLA Ops:
  0.0 1.0 copy-start
  0.0 13.4 %copy-start.3 = (s32[32,8]{0,1:T(8,128)S(1)}, s32[32,8]{0,1:T(8,128)}, u32[]{:S(2)}) copy-start(s32[32,8]{0,1:T(8,128)} %param.12) | copy-start | bytes 3076
  0.0 14.7 %copy-start.2 = (bf16[4096]{0:T(1024)(128)(2,1)S(1)}, bf16[4096]{0:T(1024)(128)(2,1)}, u32[]{:S(2)}) copy-start(bf16[4096]{0:T(1024)(128)(2,1)} %param.11) | copy-start | bytes 24580
  6.6 20.4 %copy-start.1 = (bf16[32,4096]{1,0:T(8,128)(2,1)S(1)}, bf16[32,4096]{1,0:T(8,128)(2,1)}, u32[]{:S(2)}) copy-start(bf16[32,4096]{1,0:T(8,128)(2,1)} %param.10) | copy-start | bytes 786436
  6.6 20.3 %all-to-all-start = ((bf16[4,32,4096]{2,1,0:T(8,128)(2,1)}), bf16[4,32,4096]{2,1,0:T(8,128)(2,1)S(1)}, u32[]{:S(2)}, u32[]{:S(2)}) async-start(bf16[4,32,4096]{2,1,0:T(8,128)(2,1)} %bitcast), calls=%async_computation | async-start | bytes 2097152 | tf_op jit(solution)/shard_map/all_to_all | solution.py:32
  30.5 128.8 %copy-start.8 = (bf16[1,192,4096]{2,1,0:T(8,128)(2,1)S(1)}, bf16[1,192,4096]{2,1,0:T(8,128)(2,1)}, u32[]{:S(2)}) copy-start(bf16[1,192,4096]{2,1,0:T(8,128)(2,1)} %param.15) | copy-start | bytes 4718596
  30.5 165.7 %all-to-all-start.1 = ((bf16[64,8,4096]{2,1,0:T(8,128)(2,1)}), bf16[64,8,4096]{2,1,0:T(8,128)(2,1)}, u32[]{:S(2)}, u32[]{:S(2)}) async-start(bf16[64,8,4096]{2,1,0:T(8,128)(2,1)} %fusion.11), calls=%async_computation.1 | async-start | bytes 8388608 | tf_op jit(solution)/shard_map/all_to_all | solution.py:49
  43.5 113.3 %collective-permute-start = (bf16[1,2,192,4096]{3,2,1,0:T(8,128)(2,1)}, bf16[1,2,192,4096]{3,2,1,0:T(8,128)(2,1)S(1)}, u32[]{:S(2)}, u32[]{:S(2)}) collective-permute-start(bf16[1,2,192,4096]{3,2,1,0:T(8,128)(2,1)} %param.14), channel_id=1, source_target_pairs={{0,2},{1,3},{2,0},{3,1},{4,6},{5,7},{6,4},{7,5},{8,10},{9,11},{10,... | collective-permute-start | bytes 9437192 | tf_op jit(solution)/shard_map/ppermute | solution.py:13
  156.8 1.8 copy-start.6
  158.5 37.7 %collective-permute-start.2 = (bf16[1,2,192,4096]{3,2,1,0:T(8,128)(2,1)S(1)}, bf16[1,2,192,4096]{3,2,1,0:T(8,128)(2,1)}, u32[]{:S(2)}, u32[]{:S(2)}) collective-permute-start(bf16[1,2,192,4096]{3,2,1,0:T(8,128)(2,1)S(1)} %collective-permute-done), channel_id=1, source_target_pairs={{0,1},{1,0},{2,3},{3,2},{4,5},{5,4},{6,7},{7,6},{8,9},{9,8},{10,11... | collective-permute-start | bytes 9437192 | tf_op jit(solution)/shard_map/ppermute | solution.py:17
  159.4 36.1 %collective-permute-start.3 = (bf16[1,192,4096]{2,1,0:T(8,128)(2,1)S(1)}, bf16[1,192,4096]{2,1,0:T(8,128)(2,1)}, u32[]{:S(2)}, u32[]{:S(2)}) collective-permute-start(bf16[1,192,4096]{2,1,0:T(8,128)(2,1)S(1)} %copy-done.8), channel_id=1, source_target_pairs={{0,2},{1,3},{2,0},{3,1},{4,6},{5,7},{6,4},{7,5},{8,10},{9,11},{10,... | collective-permute-start | bytes 4718600 | tf_op jit(solution)/shard_map/ppermute | solution.py:14
  160.6 45.2 %collective-permute-start.1 = (bf16[1,2,192,4096]{3,2,1,0:T(8,128)(2,1)}, bf16[1,2,192,4096]{3,2,1,0:T(8,128)(2,1)}, u32[]{:S(2)}, u32[]{:S(2)}) collective-permute-start(bf16[1,2,192,4096]{3,2,1,0:T(8,128)(2,1)} %param.14), channel_id=1, source_target_pairs={{0,1},{1,0},{2,3},{3,2},{4,5},{5,4},{6,7},{7,6},{8,9},{9,8},{10,11... | collective-permute-start | bytes 9437192 | tf_op jit(solution)/shard_map/ppermute | solution.py:16
  160.9 54.3 %collective-permute-start.4 = (bf16[1,192,4096]{2,1,0:T(8,128)(2,1)S(1)}, bf16[1,192,4096]{2,1,0:T(8,128)(2,1)}, u32[]{:S(2)}, u32[]{:S(2)}) collective-permute-start(bf16[1,192,4096]{2,1,0:T(8,128)(2,1)S(1)} %copy-done.8), channel_id=1, source_target_pairs={{0,1},{1,0},{2,3},{3,2},{4,5},{5,4},{6,7},{7,6},{8,9},{9,8},{10,11... | collective-permute-start | bytes 4718600 | tf_op jit(solution)/shard_map/ppermute | solution.py:16
  195.4 19.8 %collective-permute-start.5 = (bf16[1,192,4096]{2,1,0:T(8,128)(2,1)}, bf16[1,192,4096]{2,1,0:T(8,128)(2,1)}, u32[]{:S(2)}, u32[]{:S(2)}) collective-permute-start(bf16[1,192,4096]{2,1,0:T(8,128)(2,1)} %collective-permute-done.3), channel_id=1, source_target_pairs={{0,1},{1,0},{2,3},{3,2},{4,5},{5,4},{6,7},{7,6},{8,9},{9,8},{10,11... | collective-permute-start | bytes 4718600 | tf_op jit(solution)/shard_map/ppermute | solution.py:17
  196.3 5.3 %copy-start.7 = (bf16[1,2,192,4096]{3,2,1,0:T(8,128)(2,1)S(1)}, bf16[1,2,192,4096]{3,2,1,0:T(8,128)(2,1)}, u32[]{:S(2)}) copy-start(bf16[1,2,192,4096]{3,2,1,0:T(8,128)(2,1)} %copy-done.6) | copy-start | bytes 9437188
  205.7 5.3 %copy-start.5 = (bf16[1,2,192,4096]{3,2,1,0:T(8,128)(2,1)S(1)}, bf16[1,2,192,4096]{3,2,1,0:T(8,128)(2,1)}, u32[]{:S(2)}) copy-start(bf16[1,2,192,4096]{3,2,1,0:T(8,128)(2,1)} %param.14) | copy-start | bytes 9437188
  221.9 12.8 %copy-start.4 = (f32[32,8]{0,1:T(8,128)S(1)}, f32[32,8]{0,1:T(8,128)}, u32[]{:S(2)}) copy-start(f32[32,8]{0,1:T(8,128)} %param.13) | copy-start | bytes 3076
  221.9 106.9 %all-to-all-start.2 = ((bf16[64,8,4096]{2,1,0:T(8,128)(2,1)}), bf16[64,8,4096]{2,1,0:T(8,128)(2,1)}, u32[]{:S(2)}, u32[]{:S(2)}) async-start(bf16[64,8,4096]{2,1,0:T(8,128)(2,1)} %fusion.12), calls=%async_computation.2 | async-start | bytes 8388608 | tf_op jit(solution)/shard_map/all_to_all | solution.py:64

commit v8 on v7

--- a/solution.py
+++ b/solution.py
@@ -50,17 +50,24 @@
     received = received.reshape(ep_size, exp_local, capacity, model_width)
     slots = ep_size * exp_local * capacity
     rows = received.reshape(slots, model_width)
-    down_full = jnp.concatenate([piece.reshape(-1, model_width) for _, piece in pieces], axis=0)
     activated = []
     for gate_up_piece, _ in pieces:
         both = jnp.dot(
             rows, gate_up_piece.reshape(-1, model_width).T, preferred_element_type=jnp.float32
         ).reshape(slots, 2, -1)
         activated.append((jax.nn.silu(both[:, 0]) * both[:, 1]).astype(jnp.bfloat16))
-    activated = jnp.concatenate(activated, axis=1)
-    expert_out = jnp.dot(
-        activated, down_full, preferred_element_type=jnp.float32
-    ).astype(jnp.bfloat16)
+    downs = [piece.reshape(-1, model_width) for _, piece in pieces]
+    early_out = jnp.dot(
+        jnp.concatenate([activated[0], activated[2]], axis=1),
+        jnp.concatenate([downs[0], downs[2]], axis=0),
+        preferred_element_type=jnp.float32,
+    )
+    late_out = jnp.dot(
+        jnp.concatenate([activated[1], activated[3]], axis=1),
+        jnp.concatenate([downs[1], downs[3]], axis=0),
+        preferred_element_type=jnp.float32,
+    )
+    expert_out = (early_out + late_out).astype(jnp.bfloat16)
     returned = lax.all_to_all(
         expert_out.reshape(ep_size, exp_local * capacity, model_width),
         "ep",

time: 335 us -> 338 us (level)
  matrix products: 37 us -> 41.9 us
    dot_general x1 -> x2, matrix products: 6.66 us -> 9.96 us  [the longest x1 6.18 us: layer(): jnp.dot(jnp.concatenate([activated[1], activated[3]], axis=1), jnp.concat...]
  transfers between devices with their start and end apart: 9 -> 9, of which waited for: 4 -> 4; matrix products, arithmetic and copies ran while one was open for 6% -> 8% of each run, Pallas kernels for 0% -> 0%
where the time goes in v8:
time: 338 us; the launch traced here: 336 us
  waiting for transfers between devices  252 us (75%)
  matrix products  41.9 us (12%)
  starting transfers between devices  36.9 us (11%)
    ppermute x1, waiting for transfers between devices, gather_weights(): far_gu = lax.ppermute(w_gate_up, 'tp', far_pairs)  112 us
    all_to_all x1, waiting for transfers between devices, layer(): lax.all_to_all(expert_out.reshape(ep_size, exp_local * capacity, model_wi...  94 us
    ppermute x1, waiting for transfers between devices, gather_weights(): far_dn = lax.ppermute(w_down, 'tp', far_pairs)  34.5 us
    dot_general x4, matrix products, layer(): jnp.dot(rows, gate_up_piece.reshape(-1, model_width).T, preferred_element...  19.9 us
    all_to_all x1, starting transfers between devices, layer(): lax.all_to_all(send_rows, 'ep', split_axis=0, concat_axis=0, tiled=True)  13 us
    all_to_all x1, starting transfers between devices, layer(): lax.all_to_all(expert_out.reshape(ep_size, exp_local * capacity, model_wi...  12.5 us
    all_to_all x1, waiting for transfers between devices, layer(): lax.all_to_all(shares, 'tp', split_axis=0, concat_axis=0, tiled=True)  11.9 us
    all_to_all x1, starting transfers between devices, layer(): lax.all_to_all(shares, 'tp', split_axis=0, concat_axis=0, tiled=True)  6.81 us
  transfers between devices with their start and end apart: 9, of which 4 were waited for; matrix products, arithmetic and copies ran while one was open for 8% of the time, Pallas kernels for 0%

profile of v8, /device:TPU:1, one launch (start us, length us, event | category | flops | bytes accessed | tf_op | source)
XLA Modules:
  0.0 336.0 jit_solution(7002585917380398791)
XLA Ops:
  0.0 0.9 copy-done
  1.0 5.6 %convolution_convert_fusion.1 = bf16[128,4096]{1,0:T(8,128)(2,1)} fusion(bf16[128,1024]{1,0:T(8,128)(2,1)S(1)} %copy-done, bf16[1024,4096]{1,0:T(8,128)(2,1)} %param.9), kind=kOutput, calls=%fused_computation.4 | convolution fusion | flops 1074266112 | bytes 9699328 | tf_op jit(solution)/shard_map/dot_general | solution.py:29
  6.6 6.8 %all-to-all-start = ((bf16[4,32,4096]{2,1,0:T(8,128)(2,1)}), bf16[4,32,4096]{2,1,0:T(8,128)(2,1)S(1)}, u32[]{:S(2)}, u32[]{:S(2)}) async-start(bf16[4,32,4096]{2,1,0:T(8,128)(2,1)} %bitcast), calls=%async_computation | async-start | bytes 2097152 | tf_op jit(solution)/shard_map/all_to_all | solution.py:32
  13.7 0.6 reduce-window.6
  14.3 0.2 slice_reduce_fusion
  14.8 0.2 fusion.25
  15.0 11.9 %all-to-all-done = bf16[4,32,4096]{2,1,0:T(8,128)(2,1)S(1)} async-done(((bf16[4,32,4096]{2,1,0:T(8,128)(2,1)}), bf16[4,32,4096]{2,1,0:T(8,128)(2,1)S(1)}, u32[]{:S(2)}, u32[]{:S(2)}) %all-to-all-start) | async-done | bytes 1048608 | tf_op jit(solution)/shard_map/all_to_all | solution.py:32
  26.9 0.2 convert_reduce_fusion
  27.0 0.2 multiply_reduce_fusion
  27.2 3.3 fusion
  30.5 13.0 %all-to-all-start.1 = ((bf16[64,8,4096]{2,1,0:T(8,128)(2,1)}), bf16[64,8,4096]{2,1,0:T(8,128)(2,1)}, u32[]{:S(2)}, u32[]{:S(2)}) async-start(bf16[64,8,4096]{2,1,0:T(8,128)(2,1)} %fusion), calls=%async_computation.1 | async-start | bytes 8388608 | tf_op jit(solution)/shard_map/all_to_all | solution.py:49
  43.6 1.3 collective-permute-start
  45.0 111.9 %collective-permute-done.2 = bf16[1,2,192,4096]{3,2,1,0:T(8,128)(2,1)} collective-permute-done((bf16[1,2,192,4096]{3,2,1,0:T(8,128)(2,1)}, bf16[1,2,192,4096]{3,2,1,0:T(8,128)(2,1)}, u32[]{:S(2)}, u32[]{:S(2)}) %collective-permute-start.2) | collective-permute-done | bytes 3145760 | tf_op jit(solution)/shard_map/ppermute | solution.py:13
  156.9 0.8 collective-permute-start.3
  157.7 1.2 collective-permute-start.4
  158.9 0.3 collective-permute-start.1
  159.2 34.5 %collective-permute-done.4 = bf16[1,192,4096]{2,1,0:T(8,128)(2,1)} collective-permute-done((bf16[1,192,4096]{2,1,0:T(8,128)(2,1)S(1)}, bf16[1,192,4096]{2,1,0:T(8,128)(2,1)}, u32[]{:S(2)}, u32[]{:S(2)}) %collective-permute-start.4) | collective-permute-done | bytes 1572896 | tf_op jit(solution)/shard_map/ppermute | solution.py:14
  193.8 0.9 collective-permute-start.5
  194.6 5.0 %fusion.10 = f32[512,2,192]{0,2,1:T(8,128)S(1)} fusion(bf16[64,8,4096]{2,1,0:T(8,128)(2,1)} %all-to-all-done.1, bf16[1,2,192,4096]{3,2,1,0:T(8,128)(2,1)} %param.14), kind=kOutput, calls=%fused_computation.13 | convolution fusion | flops 1610612736 | bytes 8126464 | tf_op jit(solution)/shard_map/dot_general | solution.py:55
  199.6 5.0 %fusion.8 = f32[512,2,192]{0,2,1:T(8,128)S(1)} fusion(bf16[64,8,4096]{2,1,0:T(8,128)(2,1)} %all-to-all-done.1, bf16[1,2,192,4096]{3,2,1,0:T(8,128)(2,1)} %collective-permute-done), kind=kOutput, calls=%fused_computation.11 | convolution fusion | flops 1610612736 | bytes 8126464 | tf_op jit(solution)/shard_map/dot_general | solution.py:55
  204.6 5.0 %fusion.4 = f32[512,2,192]{0,2,1:T(8,128)S(1)} fusion(bf16[64,8,4096]{2,1,0:T(8,128)(2,1)} %all-to-all-done.1, bf16[1,2,192,4096]{3,2,1,0:T(8,128)(2,1)} %collective-permute-done.3), kind=kOutput, calls=%fused_computation.7 | convolution fusion | flops 1610612736 | bytes 8126464 | tf_op jit(solution)/shard_map/dot_general | solution.py:55
  209.6 0.1 fusion.31
  209.7 0.1 fusion.33
  210.0 5.0 %fusion.6 = f32[512,2,192]{0,2,1:T(8,128)S(1)} fusion(bf16[64,8,4096]{2,1,0:T(8,128)(2,1)} %all-to-all-done.1, bf16[1,2,192,4096]{3,2,1,0:T(8,128)(2,1)} %collective-permute-done.2), kind=kOutput, calls=%fused_computation.9 | convolution fusion | flops 1610612736 | bytes 8126464 | tf_op jit(solution)/shard_map/dot_general | solution.py:55
  215.1 3.8 %fusion.12 = f32[512,4096]{1,0:T(8,128)S(1)} fusion(bf16[192,4096]{1,0:T(8,128)(2,1)} %bitcast.21, bf16[192,4096]{1,0:T(8,128)(2,1)S(1)} %bitcast.113, bf16[512,192]{0,1:T(8,128)(2,1)S(1)} %fusion.31, bf16[512,192]{0,1:T(8,128)(2,1)S(1)} %fusion.33), kind=kOutput, calls=%fused_computation.15 | convolution fusion | flops 1617690624 | bytes 11927552 | tf_op jit(solution)/shard_map/dot_general | solution.py:60
  218.9 6.2 %fusion.1 = bf16[64,8,4096]{2,1,0:T(8,128)(2,1)} fusion(f32[512,4096]{1,0:T(8,128)S(1)} %fusion.12, bf16[192,4096]{1,0:T(8,128)(2,1)} %bitcast.29, bf16[192,4096]{1,0:T(8,128)(2,1)} %bitcast.28, bf16[512,192]{0,1:T(8,128)(2,1)S(1)} %fusion.27, bf16[512,192]{0,1:T(8,128)(2,1)S(1)} %fusion.29), kind=kOutput, calls=%fused_computation.3 | convolution fusion | flops 1621884928 | bytes 16121856 | tf_op jit(solution)/shard_map/dot_general | solution.py:65
  225.1 12.5 %all-to-all-start.2 = ((bf16[64,8,4096]{2,1,0:T(8,128)(2,1)}), bf16[64,8,4096]{2,1,0:T(8,128)(2,1)}, u32[]{:S(2)}, u32[]{:S(2)}) async-start(bf16[64,8,4096]{2,1,0:T(8,128)(2,1)} %fusion.1), calls=%async_computation.2 | async-start | bytes 8388608 | tf_op jit(solution)/shard_map/all_to_all | solution.py:71
  237.6 0.3 slice_reduce_fusion.8
  237.9 0.1 subtract_convert_fusion
  238.1 94.0 %all-to-all-done.2 = bf16[64,8,4096]{2,1,0:T(8,128)(2,1)} async-done(((bf16[64,8,4096]{2,1,0:T(8,128)(2,1)}), bf16[64,8,4096]{2,1,0:T(8,128)(2,1)}, u32[]{:S(2)}, u32[]{:S(2)}) %all-to-all-start.2) | async-done | bytes 4194336 | tf_op jit(solution)/shard_map/all_to_all | solution.py:71
  332.1 3.0 fusion.2
  335.1 0.8 fusion.24
  (31 shorter events, 0.9 us)
Async XLA Ops:
  0.0 1.0 copy-start
  0.0 13.4 %copy-start.4 = (s32[32,8]{0,1:T(8,128)S(1)}, s32[32,8]{0,1:T(8,128)}, u32[]{:S(2)}) copy-start(s32[32,8]{0,1:T(8,128)} %param.12) | copy-start | bytes 3076
  0.0 14.7 %copy-start.3 = (bf16[4096]{0:T(1024)(128)(2,1)S(1)}, bf16[4096]{0:T(1024)(128)(2,1)}, u32[]{:S(2)}) copy-start(bf16[4096]{0:T(1024)(128)(2,1)} %param.11) | copy-start | bytes 24580
  6.6 20.4 %copy-start.1 = (bf16[32,4096]{1,0:T(8,128)(2,1)S(1)}, bf16[32,4096]{1,0:T(8,128)(2,1)}, u32[]{:S(2)}) copy-start(bf16[32,4096]{1,0:T(8,128)(2,1)} %param.10) | copy-start | bytes 786436
  6.6 20.3 %all-to-all-start = ((bf16[4,32,4096]{2,1,0:T(8,128)(2,1)}), bf16[4,32,4096]{2,1,0:T(8,128)(2,1)S(1)}, u32[]{:S(2)}, u32[]{:S(2)}) async-start(bf16[4,32,4096]{2,1,0:T(8,128)(2,1)} %bitcast), calls=%async_computation | async-start | bytes 2097152 | tf_op jit(solution)/shard_map/all_to_all | solution.py:32
  30.5 127.2 %copy-start.2 = (bf16[1,192,4096]{2,1,0:T(8,128)(2,1)S(1)}, bf16[1,192,4096]{2,1,0:T(8,128)(2,1)}, u32[]{:S(2)}) copy-start(bf16[1,192,4096]{2,1,0:T(8,128)(2,1)} %param.15) | copy-start | bytes 4718596
  30.5 164.1 %all-to-all-start.1 = ((bf16[64,8,4096]{2,1,0:T(8,128)(2,1)}), bf16[64,8,4096]{2,1,0:T(8,128)(2,1)}, u32[]{:S(2)}, u32[]{:S(2)}) async-start(bf16[64,8,4096]{2,1,0:T(8,128)(2,1)} %fusion), calls=%async_computation.1 | async-start | bytes 8388608 | tf_op jit(solution)/shard_map/all_to_all | solution.py:49
  43.5 113.4 %collective-permute-start.2 = (bf16[1,2,192,4096]{3,2,1,0:T(8,128)(2,1)}, bf16[1,2,192,4096]{3,2,1,0:T(8,128)(2,1)}, u32[]{:S(2)}, u32[]{:S(2)}) collective-permute-start(bf16[1,2,192,4096]{3,2,1,0:T(8,128)(2,1)} %param.14), channel_id=1, source_target_pairs={{0,2},{1,3},{2,0},{3,1},{4,6},{5,7},{6,4},{7,5},{8,10},{9,11},{10,... | collective-permute-start | bytes 9437192 | tf_op jit(solution)/shard_map/ppermute | solution.py:13
  43.6 156.0 %collective-permute-start = (bf16[1,2,192,4096]{3,2,1,0:T(8,128)(2,1)}, bf16[1,2,192,4096]{3,2,1,0:T(8,128)(2,1)}, u32[]{:S(2)}, u32[]{:S(2)}) collective-permute-start(bf16[1,2,192,4096]{3,2,1,0:T(8,128)(2,1)} %param.14), channel_id=1, source_target_pairs={{0,1},{1,0},{2,3},{3,2},{4,5},{5,4},{6,7},{7,6},{8,9},{9,8},{10,11... | collective-permute-start | bytes 9437192 | tf_op jit(solution)/shard_map/ppermute | solution.py:16
  156.9 47.7 %collective-permute-start.3 = (bf16[1,2,192,4096]{3,2,1,0:T(8,128)(2,1)}, bf16[1,2,192,4096]{3,2,1,0:T(8,128)(2,1)}, u32[]{:S(2)}, u32[]{:S(2)}) collective-permute-start(bf16[1,2,192,4096]{3,2,1,0:T(8,128)(2,1)} %collective-permute-done.2), channel_id=1, source_target_pairs={{0,1},{1,0},{2,3},{3,2},{4,5},{5,4},{6,7},{7,6},{8,9},{9,8},{10,11... | collective-permute-start | bytes 9437192 | tf_op jit(solution)/shard_map/ppermute | solution.py:17
  157.7 36.1 %collective-permute-start.4 = (bf16[1,192,4096]{2,1,0:T(8,128)(2,1)S(1)}, bf16[1,192,4096]{2,1,0:T(8,128)(2,1)}, u32[]{:S(2)}, u32[]{:S(2)}) collective-permute-start(bf16[1,192,4096]{2,1,0:T(8,128)(2,1)S(1)} %copy-done.2), channel_id=1, source_target_pairs={{0,2},{1,3},{2,0},{3,1},{4,6},{5,7},{6,4},{7,5},{8,10},{9,11},{10,... | collective-permute-start | bytes 4718600 | tf_op jit(solution)/shard_map/ppermute | solution.py:14
  158.9 56.2 %collective-permute-start.1 = (bf16[1,192,4096]{2,1,0:T(8,128)(2,1)S(1)}, bf16[1,192,4096]{2,1,0:T(8,128)(2,1)}, u32[]{:S(2)}, u32[]{:S(2)}) collective-permute-start(bf16[1,192,4096]{2,1,0:T(8,128)(2,1)S(1)} %copy-done.2), channel_id=1, source_target_pairs={{0,1},{1,0},{2,3},{3,2},{4,5},{5,4},{6,7},{7,6},{8,9},{9,8},{10,11... | collective-permute-start | bytes 4718600 | tf_op jit(solution)/shard_map/ppermute | solution.py:16
  193.8 25.2 %collective-permute-start.5 = (bf16[1,192,4096]{2,1,0:T(8,128)(2,1)}, bf16[1,192,4096]{2,1,0:T(8,128)(2,1)}, u32[]{:S(2)}, u32[]{:S(2)}) collective-permute-start(bf16[1,192,4096]{2,1,0:T(8,128)(2,1)} %collective-permute-done.4), channel_id=1, source_target_pairs={{0,1},{1,0},{2,3},{3,2},{4,5},{5,4},{6,7},{7,6},{8,9},{9,8},{10,11... | collective-permute-start | bytes 4718600 | tf_op jit(solution)/shard_map/ppermute | solution.py:17
  225.1 12.8 %copy-start.5 = (f32[32,8]{0,1:T(8,128)S(1)}, f32[32,8]{0,1:T(8,128)}, u32[]{:S(2)}) copy-start(f32[32,8]{0,1:T(8,128)} %param.13) | copy-start | bytes 3076
  225.1 107.0 %all-to-all-start.2 = ((bf16[64,8,4096]{2,1,0:T(8,128)(2,1)}), bf16[64,8,4096]{2,1,0:T(8,128)(2,1)}, u32[]{:S(2)}, u32[]{:S(2)}) async-start(bf16[64,8,4096]{2,1,0:T(8,128)(2,1)} %fusion.1), calls=%async_computation.2 | async-start | bytes 8388608 | tf_op jit(solution)/shard_map/all_to_all | solution.py:71

commit v9 on v8

--- a/solution.py
+++ b/solution.py
@@ -50,20 +50,22 @@
     received = received.reshape(ep_size, exp_local, capacity, model_width)
     slots = ep_size * exp_local * capacity
     rows = received.reshape(slots, model_width)
-    activated = []
-    for gate_up_piece, _ in pieces:
-        both = jnp.dot(
-            rows, gate_up_piece.reshape(-1, model_width).T, preferred_element_type=jnp.float32
-        ).reshape(slots, 2, -1)
-        activated.append((jax.nn.silu(both[:, 0]) * both[:, 1]).astype(jnp.bfloat16))
+    def gate_up_of(chosen):
+        weight = jnp.concatenate([piece.reshape(-1, model_width) for piece in chosen], axis=0)
+        both = jnp.dot(rows, weight.T, preferred_element_type=jnp.float32)
+        both = both.reshape(slots, len(chosen), 2, -1)
+        return (jax.nn.silu(both[:, :, 0]) * both[:, :, 1]).astype(jnp.bfloat16).reshape(slots, -1)
+
+    early_act = gate_up_of([pieces[0][0], pieces[2][0]])
+    late_act = gate_up_of([pieces[1][0], pieces[3][0]])
     downs = [piece.reshape(-1, model_width) for _, piece in pieces]
     early_out = jnp.dot(
-        jnp.concatenate([activated[0], activated[2]], axis=1),
+        early_act,
         jnp.concatenate([downs[0], downs[2]], axis=0),
         preferred_element_type=jnp.float32,
     )
     late_out = jnp.dot(
-        jnp.concatenate([activated[1], activated[3]], axis=1),
+        late_act,
         jnp.concatenate([downs[1], downs[3]], axis=0),
         preferred_element_type=jnp.float32,
     )

time: 338 us -> 340 us (level)
  other arithmetic: 2.81 us -> 11.6 us
  matrix products: 41.9 us -> 34.2 us
    concatenate x0 -> x2, other arithmetic: none -> 8.8 us  [gate_up_of(): jnp.concatenate([piece.reshape(-1, model_width) for piece in chosen], axi...]
    dot_general x6 -> x4, matrix products: 29.9 us -> 22.3 us  [the longest x2 12.4 us: gate_up_of(): both = jnp.dot(rows, weight.T, preferred_element_type=jnp.float32)]
where the time goes in v9:
time: 340 us; the launch traced here: 338 us
  waiting for transfers between devices  253 us (74%)
  starting transfers between devices  36.8 us (11%)
  matrix products  34.2 us (10%)
  other arithmetic  11.6 us (3%)
    ppermute x1, waiting for transfers between devices, gather_weights(): far_gu = lax.ppermute(w_gate_up, 'tp', far_pairs)  112 us
    all_to_all x1, waiting for transfers between devices, layer(): lax.all_to_all(expert_out.reshape(ep_size, exp_local * capacity, model_wi...  94.1 us
    ppermute x1, waiting for transfers between devices, gather_weights(): far_dn = lax.ppermute(w_down, 'tp', far_pairs)  34.7 us
    all_to_all x1, starting transfers between devices, layer(): lax.all_to_all(send_rows, 'ep', split_axis=0, concat_axis=0, tiled=True)  12.8 us
    all_to_all x1, starting transfers between devices, layer(): lax.all_to_all(expert_out.reshape(ep_size, exp_local * capacity, model_wi...  12.5 us
    dot_general x2, matrix products, gate_up_of(): both = jnp.dot(rows, weight.T, preferred_element_type=jnp.float32)  12.4 us
    all_to_all x1, waiting for transfers between devices, layer(): lax.all_to_all(shares, 'tp', split_axis=0, concat_axis=0, tiled=True)  11.9 us
    concatenate x2, other arithmetic, gate_up_of(): jnp.concatenate([piece.reshape(-1, model_width) for piece in chosen], axi...  8.8 us
  transfers between devices with their start and end apart: 9, of which 4 were waited for; matrix products, arithmetic and copies ran while one was open for 8% of the time, Pallas kernels for 0%

profile of v9, /device:TPU:1, one launch (start us, length us, event | category | flops | bytes accessed | tf_op | source)
XLA Modules:
  0.0 338.1 jit_solution(1140416510135479554)
XLA Ops:
  0.0 0.9 copy-done
  1.0 5.6 %convolution_convert_fusion.1 = bf16[128,4096]{1,0:T(8,128)(2,1)} fusion(bf16[128,1024]{1,0:T(8,128)(2,1)S(1)} %copy-done, bf16[1024,4096]{1,0:T(8,128)(2,1)} %param.9), kind=kOutput, calls=%fused_computation.6 | convolution fusion | flops 1074266112 | bytes 9699328 | tf_op jit(solution)/shard_map/dot_general | solution.py:29
  6.6 6.8 %all-to-all-start = ((bf16[4,32,4096]{2,1,0:T(8,128)(2,1)}), bf16[4,32,4096]{2,1,0:T(8,128)(2,1)S(1)}, u32[]{:S(2)}, u32[]{:S(2)}) async-start(bf16[4,32,4096]{2,1,0:T(8,128)(2,1)} %bitcast), calls=%async_computation | async-start | bytes 2097152 | tf_op jit(solution)/shard_map/all_to_all | solution.py:32
  13.7 0.6 reduce-window.6
  14.3 0.2 slice_reduce_fusion
  14.8 0.2 fusion.25
  15.0 11.9 %all-to-all-done = bf16[4,32,4096]{2,1,0:T(8,128)(2,1)S(1)} async-done(((bf16[4,32,4096]{2,1,0:T(8,128)(2,1)}), bf16[4,32,4096]{2,1,0:T(8,128)(2,1)S(1)}, u32[]{:S(2)}, u32[]{:S(2)}) %all-to-all-start) | async-done | bytes 1048608 | tf_op jit(solution)/shard_map/all_to_all | solution.py:32
  26.9 0.2 convert_reduce_fusion
  27.0 0.2 multiply_reduce_fusion
  27.2 3.2 fusion
  30.5 12.8 %all-to-all-start.1 = ((bf16[64,8,4096]{2,1,0:T(8,128)(2,1)}), bf16[64,8,4096]{2,1,0:T(8,128)(2,1)}, u32[]{:S(2)}, u32[]{:S(2)}) async-start(bf16[64,8,4096]{2,1,0:T(8,128)(2,1)} %fusion), calls=%async_computation.1 | async-start | bytes 8388608 | tf_op jit(solution)/shard_map/all_to_all | solution.py:49
  43.4 1.3 collective-permute-start
  44.8 111.8 %collective-permute-done.2 = bf16[1,2,192,4096]{3,2,1,0:T(8,128)(2,1)S(1)} collective-permute-done((bf16[1,2,192,4096]{3,2,1,0:T(8,128)(2,1)}, bf16[1,2,192,4096]{3,2,1,0:T(8,128)(2,1)S(1)}, u32[]{:S(2)}, u32[]{:S(2)}) %collective-permute-start.2) | collective-permute-done | bytes 3145760 | tf_op jit(solution)/shard_map/ppermute | solution.py:13
  156.6 0.8 collective-permute-start.3
  157.4 1.2 collective-permute-start.4
  158.7 0.3 collective-permute-start.1
  158.9 34.7 %collective-permute-done.4 = bf16[1,192,4096]{2,1,0:T(8,128)(2,1)} collective-permute-done((bf16[1,192,4096]{2,1,0:T(8,128)(2,1)}, bf16[1,192,4096]{2,1,0:T(8,128)(2,1)}, u32[]{:S(2)}, u32[]{:S(2)}) %collective-permute-start.4) | collective-permute-done | bytes 1572896 | tf_op jit(solution)/shard_map/ppermute | solution.py:14
  193.7 0.9 collective-permute-start.5
  194.5 5.3 %pad_maximum_fusion = bf16[768,4096]{1,0:T(8,128)(2,1)} fusion(bf16[384,4096]{1,0:T(8,128)(2,1)S(1)} %bitcast.107, bf16[384,4096]{1,0:T(8,128)(2,1)} %bitcast.105), kind=kLoop, calls=%fused_computation.1 | loop fusion | flops 12582912 | bytes 12582912 | tf_op jit(solution)/shard_map/concatenate | solution.py:54
  199.9 3.5 %pad_maximum_fusion.1 = bf16[768,4096]{1,0:T(8,128)(2,1)} fusion(bf16[384,4096]{1,0:T(8,128)(2,1)S(1)} %bitcast.108, bf16[384,4096]{1,0:T(8,128)(2,1)S(1)} %bitcast.106), kind=kLoop, calls=%fused_computation.2 | loop fusion | flops 12582912 | bytes 12582912 | tf_op jit(solution)/shard_map/concatenate | solution.py:54
  203.4 7.0 %fusion.4 = f32[512,2,2,192]{0,3,2,1:T(8,128)S(1)} fusion(bf16[2,2,192,4096]{3,2,1,0:T(8,128)(2,1)} %bitcast.104, bf16[64,8,4096]{2,1,0:T(8,128)(2,1)} %all-to-all-done.1), kind=kOutput, calls=%fused_computation.9 | convolution fusion | flops 3221225472 | bytes 12058624 | tf_op jit(solution)/shard_map/dot_general | solution.py:55
  210.3 5.4 %fusion.6 = f32[512,2,2,192]{0,3,2,1:T(8,128)S(1)} fusion(bf16[2,2,192,4096]{3,2,1,0:T(8,128)(2,1)S(1)} %bitcast.103, bf16[64,8,4096]{2,1,0:T(8,128)(2,1)} %all-to-all-done.1), kind=kOutput, calls=%fused_computation.11 | convolution fusion | flops 3221225472 | bytes 12058624 | tf_op jit(solution)/shard_map/dot_general | solution.py:55
  215.9 0.2 fusion.15
  216.3 0.2 fusion.19
  216.5 0.8 copy-done.4
  217.3 3.8 %fusion.8 = f32[512,4096]{1,0:T(8,128)S(1)} fusion(bf16[512,384]{0,1:T(8,128)(2,1)S(1)} %fusion.19, bf16[192,4096]{1,0:T(8,128)(2,1)} %bitcast.20, bf16[192,4096]{1,0:T(8,128)(2,1)S(1)} %bitcast.109), kind=kOutput, calls=%fused_computation.13 | convolution fusion | flops 1616904192 | bytes 11927552 | tf_op jit(solution)/shard_map/dot_general | solution.py:62
  221.1 6.2 %fusion.1 = bf16[64,8,4096]{2,1,0:T(8,128)(2,1)} fusion(f32[512,4096]{1,0:T(8,128)S(1)} %fusion.8, bf16[512,384]{0,1:T(8,128)(2,1)S(1)} %fusion.15, bf16[192,4096]{1,0:T(8,128)(2,1)} %bitcast.29, bf16[192,4096]{1,0:T(8,128)(2,1)} %bitcast.28), kind=kOutput, calls=%fused_computation.5 | convolution fusion | flops 1621098496 | bytes 16121856 | tf_op jit(solution)/shard_map/dot_general | solution.py:67
  227.3 12.5 %all-to-all-start.2 = ((bf16[64,8,4096]{2,1,0:T(8,128)(2,1)}), bf16[64,8,4096]{2,1,0:T(8,128)(2,1)}, u32[]{:S(2)}, u32[]{:S(2)}) async-start(bf16[64,8,4096]{2,1,0:T(8,128)(2,1)} %fusion.1), calls=%async_computation.2 | async-start | bytes 8388608 | tf_op jit(solution)/shard_map/all_to_all | solution.py:73
  239.8 0.3 slice_reduce_fusion.8
  240.2 94.1 %all-to-all-done.2 = bf16[64,8,4096]{2,1,0:T(8,128)(2,1)} async-done(((bf16[64,8,4096]{2,1,0:T(8,128)(2,1)}), bf16[64,8,4096]{2,1,0:T(8,128)(2,1)}, u32[]{:S(2)}, u32[]{:S(2)}) %all-to-all-start.2) | async-done | bytes 4194336 | tf_op jit(solution)/shard_map/all_to_all | solution.py:73
  334.3 3.0 fusion.2
  337.3 0.8 fusion.24
  (35 shorter events, 1.1 us)
Async XLA Ops:
  0.0 1.0 copy-start
  0.0 13.4 %copy-start.6 = (s32[32,8]{0,1:T(8,128)S(1)}, s32[32,8]{0,1:T(8,128)}, u32[]{:S(2)}) copy-start(s32[32,8]{0,1:T(8,128)} %param.12) | copy-start | bytes 3076
  0.0 14.7 %copy-start.5 = (bf16[4096]{0:T(1024)(128)(2,1)S(1)}, bf16[4096]{0:T(1024)(128)(2,1)}, u32[]{:S(2)}) copy-start(bf16[4096]{0:T(1024)(128)(2,1)} %param.11) | copy-start | bytes 24580
  6.6 20.4 %copy-start.3 = (bf16[32,4096]{1,0:T(8,128)(2,1)S(1)}, bf16[32,4096]{1,0:T(8,128)(2,1)}, u32[]{:S(2)}) copy-start(bf16[32,4096]{1,0:T(8,128)(2,1)} %param.10) | copy-start | bytes 786436
  6.6 20.3 %all-to-all-start = ((bf16[4,32,4096]{2,1,0:T(8,128)(2,1)}), bf16[4,32,4096]{2,1,0:T(8,128)(2,1)S(1)}, u32[]{:S(2)}, u32[]{:S(2)}) async-start(bf16[4,32,4096]{2,1,0:T(8,128)(2,1)} %bitcast), calls=%async_computation | async-start | bytes 2097152 | tf_op jit(solution)/shard_map/all_to_all | solution.py:32
  30.5 172.9 %all-to-all-start.1 = ((bf16[64,8,4096]{2,1,0:T(8,128)(2,1)}), bf16[64,8,4096]{2,1,0:T(8,128)(2,1)}, u32[]{:S(2)}, u32[]{:S(2)}) async-start(bf16[64,8,4096]{2,1,0:T(8,128)(2,1)} %fusion), calls=%async_computation.1 | async-start | bytes 8388608 | tf_op jit(solution)/shard_map/all_to_all | solution.py:49
  43.3 113.3 %collective-permute-start.2 = (bf16[1,2,192,4096]{3,2,1,0:T(8,128)(2,1)}, bf16[1,2,192,4096]{3,2,1,0:T(8,128)(2,1)S(1)}, u32[]{:S(2)}, u32[]{:S(2)}) collective-permute-start(bf16[1,2,192,4096]{3,2,1,0:T(8,128)(2,1)} %param.14), channel_id=1, source_target_pairs={{0,2},{1,3},{2,0},{3,1},{4,6},{5,7},{6,4},{7,5},{8,10},{9,11},{10,... | collective-permute-start | bytes 9437192 | tf_op jit(solution)/shard_map/ppermute | solution.py:13
  43.4 151.1 %collective-permute-start = (bf16[1,2,192,4096]{3,2,1,0:T(8,128)(2,1)}, bf16[1,2,192,4096]{3,2,1,0:T(8,128)(2,1)S(1)}, u32[]{:S(2)}, u32[]{:S(2)}) collective-permute-start(bf16[1,2,192,4096]{3,2,1,0:T(8,128)(2,1)} %param.14), channel_id=1, source_target_pairs={{0,1},{1,0},{2,3},{3,2},{4,5},{5,4},{6,7},{7,6},{8,9},{9,8},{10,11... | collective-permute-start | bytes 9437192 | tf_op jit(solution)/shard_map/ppermute | solution.py:16
  156.6 43.3 %collective-permute-start.3 = (bf16[1,2,192,4096]{3,2,1,0:T(8,128)(2,1)S(1)}, bf16[1,2,192,4096]{3,2,1,0:T(8,128)(2,1)S(1)}, u32[]{:S(2)}, u32[]{:S(2)}) collective-permute-start(bf16[1,2,192,4096]{3,2,1,0:T(8,128)(2,1)S(1)} %collective-permute-done.2), channel_id=1, source_target_pairs={{0,1},{1,0},{2,3},{3,2},{4,5},{5,4},{6,7},{7,6},{8,9},{9,8},{10,11... | collective-permute-start | bytes 9437192 | tf_op jit(solution)/shard_map/ppermute | solution.py:17
  157.4 36.3 %collective-permute-start.4 = (bf16[1,192,4096]{2,1,0:T(8,128)(2,1)}, bf16[1,192,4096]{2,1,0:T(8,128)(2,1)}, u32[]{:S(2)}, u32[]{:S(2)}) collective-permute-start(bf16[1,192,4096]{2,1,0:T(8,128)(2,1)} %param.15), channel_id=1, source_target_pairs={{0,2},{1,3},{2,0},{3,1},{4,6},{5,7},{6,4},{7,5},{8,10},{9,11},{10,... | collective-permute-start | bytes 4718600 | tf_op jit(solution)/shard_map/ppermute | solution.py:14
  158.7 57.9 %collective-permute-start.1 = (bf16[1,192,4096]{2,1,0:T(8,128)(2,1)}, bf16[1,192,4096]{2,1,0:T(8,128)(2,1)}, u32[]{:S(2)}, u32[]{:S(2)}) collective-permute-start(bf16[1,192,4096]{2,1,0:T(8,128)(2,1)} %param.15), channel_id=1, source_target_pairs={{0,1},{1,0},{2,3},{3,2},{4,5},{5,4},{6,7},{7,6},{8,9},{9,8},{10,11... | collective-permute-start | bytes 4718600 | tf_op jit(solution)/shard_map/ppermute | solution.py:16
  193.7 27.4 %collective-permute-start.5 = (bf16[1,192,4096]{2,1,0:T(8,128)(2,1)}, bf16[1,192,4096]{2,1,0:T(8,128)(2,1)}, u32[]{:S(2)}, u32[]{:S(2)}) collective-permute-start(bf16[1,192,4096]{2,1,0:T(8,128)(2,1)} %collective-permute-done.4), channel_id=1, source_target_pairs={{0,1},{1,0},{2,3},{3,2},{4,5},{5,4},{6,7},{7,6},{8,9},{9,8},{10,11... | collective-permute-start | bytes 4718600 | tf_op jit(solution)/shard_map/ppermute | solution.py:17
  203.4 7.0 %copy-start.2 = (bf16[768,4096]{1,0:T(8,128)(2,1)S(1)}, bf16[768,4096]{1,0:T(8,128)(2,1)}, u32[]{:S(2)}) copy-start(bf16[768,4096]{1,0:T(8,128)(2,1)} %pad_maximum_fusion) | copy-start | bytes 18874372
  215.9 1.4 copy-start.4
  227.3 12.8 %copy-start.7 = (f32[32,8]{0,1:T(8,128)S(1)}, f32[32,8]{0,1:T(8,128)}, u32[]{:S(2)}) copy-start(f32[32,8]{0,1:T(8,128)} %param.13) | copy-start | bytes 3076
  227.3 107.0 %all-to-all-start.2 = ((bf16[64,8,4096]{2,1,0:T(8,128)(2,1)}), bf16[64,8,4096]{2,1,0:T(8,128)(2,1)}, u32[]{:S(2)}, u32[]{:S(2)}) async-start(bf16[64,8,4096]{2,1,0:T(8,128)(2,1)} %fusion.1), calls=%async_computation.2 | async-start | bytes 8388608 | tf_op jit(solution)/shard_map/all_to_all | solution.py:73
  239.7 98.4 %copy-start.1 = (bf16[128,1024]{1,0:T(8,128)(2,1)S(1)}, bf16[128,1024]{1,0:T(8,128)(2,1)}, u32[]{:S(2)}) copy-start(bf16[128,1024]{1,0:T(8,128)(2,1)} %param.8) | copy-start | bytes 786436
